TPU v7x, 32 devices: a whole 2x2x4 slice. The times are simulated.
32 devices in a mesh: dp: 4 (over y, x), section: 2 (over core), tensor: 4 (over z).
Axes of the slice: x: 2, y: 2, z: 4, core: 2. Of those that a mesh axis runs over, the one named last changes fastest.
Arguments:
- in_delta: bfloat16 [8, 1024, 4096], P(None, ('dp', 'tensor')), may hold values from -12 to 12
- weight: bfloat16 [2, 4096, 4096], P('section', 'tensor'), may hold values from -0.09375 to 0.09375
- cache_codes: int32 [2, 2, 8, 1024, 4096], P('section', None, None, ('dp', 'tensor')), may hold values from -7 to 7, as said below
- cache_scales: float32 [2, 2, 8, 4, 32], P('section', None, None, 'dp'), may hold values from 0.2 to 6, as said below
- cotangent: bfloat16 [8, 1024, 4096], P(None, ('dp', 'tensor')), may hold values from -6 to 6
Outputs:
- out_deltas: bfloat16 [2, 8, 1024, 4096], P('section', None, ('dp', 'tensor'))
- grad_in: bfloat16 [2, 8, 1024, 4096], P('section', None, ('dp', 'tensor'))
- weight_grad: float32 [2, 4096, 4096], P('section', 'tensor', 'dp')
Inputs may be any that keep to these rules, and one draw needn't show every extreme that they name: cache_codes[s, 1] equals cache_codes[s + 1, 0]: the buffer of a boundary between two segments is held by both. cache_scales[s, 1] equals cache_scales[s + 1, 0].
All inputs are finite; a program needn't handle non-finite values. Where the computation divides by a largest or mean magnitude, that divisor is 1e-20 or more.
Results may differ from a plain program's by a relative error of at most 0.013.
Values may be sent and summed in bfloat16 or wider, within the bound.
A program may use at most 320 MiB of HBM per device.

v0:
```python
import jax
import jax.numpy as jnp
from jax import lax
from jax.sharding import PartitionSpec as P

code_levels = 7.0
softness = 0.8
two_pi = 6.283185307179586
epsilon = 1e-06


def from_behind(value, axis, steps):
    count = lax.axis_size(axis)
    initial, last = (max(0, -steps), min(count, count - steps))
    return lax.ppermute(value, axis, [(source, source + steps) for source in range(initial, last)])


def dequantize(stored_codes, scales_row):
    row_count = stored_codes.shape[0]
    count_blocks = scales_row.shape[-1]
    blocked = stored_codes.astype(jnp.float32).reshape(row_count, count_blocks, -1)
    return (blocked * scales_row[None, :, None] / code_levels).reshape(row_count, -1)


def soft_codes(boundary_delta, merged):
    row_count = boundary_delta.shape[0]
    blocked = boundary_delta.reshape(row_count, merged.shape[0], -1)
    spread = merged[None, :, None]
    level_value = code_levels * blocked / spread
    smooth = level_value - softness * jnp.sin(two_pi * level_value) / two_pi
    return (smooth * spread / code_levels).astype(jnp.bfloat16).reshape(row_count, -1)


def inverse_rms(hidden):
    return lax.rsqrt(jnp.mean(hidden * hidden, axis=-1, keepdims=True) + epsilon)


def store_slot(buffer, new_value, slot_index, active):
    updated = lax.dynamic_update_index_in_dim(buffer, new_value, slot_index, 0)
    return jnp.where(active, updated, buffer)


def local(in_delta, weight, cache_codes, cache_scales, cotangent):
    segment_count = lax.axis_size("section")
    segment_index = lax.axis_index("section")
    micro_count = in_delta.shape[0]
    local_rows = in_delta.shape[1]
    model_width = in_delta.shape[2]
    weight_block = weight[0]
    block_width = weight_block.shape[0]
    full_rows = local_rows * lax.axis_size("tensor")
    tick_count = micro_count + segment_count - 1
    buffers = {
        "send_forward": jnp.zeros((local_rows, model_width), jnp.bfloat16),
        "send_backward": jnp.zeros((local_rows, model_width), jnp.bfloat16),
        "hidden_saved": jnp.zeros((micro_count, local_rows, model_width), jnp.float32),
        "normed_saved": jnp.zeros((micro_count, full_rows, block_width), jnp.bfloat16),
        "deltas_out": jnp.zeros((micro_count, local_rows, model_width), jnp.bfloat16),
        "grads_out": jnp.zeros((micro_count, local_rows, model_width), jnp.bfloat16),
        "weight_total": jnp.zeros((block_width, model_width), jnp.float32),
    }

    def forward_tick(tick_now):
        micro_now = tick_now - segment_index
        active = (micro_now >= 0) & (micro_now < micro_count)
        slot_index = jnp.clip(micro_now, 0, micro_count - 1)
        if tick_now == 0:
            received = jnp.zeros_like(buffers["send_forward"])
        else:
            received = from_behind(buffers["send_forward"], "section", 1)
        incoming = jnp.where(
            segment_index == 0,
            lax.dynamic_index_in_dim(in_delta, slot_index, 0, keepdims=False),
            received,
        )
        codes_now = lax.dynamic_index_in_dim(cache_codes[0], slot_index, 1, keepdims=False)
        scales_now = lax.dynamic_index_in_dim(cache_scales[0], slot_index, 1, keepdims=False)
        hidden = dequantize(codes_now[0], scales_now[0, 0]) + incoming.astype(jnp.float32)
        normed = (hidden * inverse_rms(hidden)).astype(jnp.bfloat16)
        normed_cols = lax.all_to_all(normed, "tensor", split_axis=1, concat_axis=0, tiled=True)
        branch = lax.psum_scatter(
            jnp.dot(normed_cols, weight_block, preferred_element_type=jnp.float32).astype(
                jnp.bfloat16
            ),
            "tensor",
            scatter_dimension=0,
            tiled=True,
        ).astype(jnp.float32)
        boundary_delta = hidden + branch - dequantize(codes_now[1], scales_now[1, 0])
        block_count = scales_now.shape[-1]
        local_peak = jnp.max(
            jnp.abs(boundary_delta).reshape(local_rows, block_count, -1), axis=(0, 2)
        )
        merged = lax.pmax(local_peak, "tensor") + epsilon
        sent_values = soft_codes(boundary_delta, merged)
        buffers["send_forward"] = sent_values
        buffers["deltas_out"] = store_slot(buffers["deltas_out"], sent_values, slot_index, active)
        buffers["hidden_saved"] = store_slot(buffers["hidden_saved"], hidden, slot_index, active)
        buffers["normed_saved"] = store_slot(
            buffers["normed_saved"], normed_cols, slot_index, active
        )

    def backward_tick(tick_back):
        micro_now = tick_back - (segment_count - 1 - segment_index)
        active = (micro_now >= 0) & (micro_now < micro_count)
        slot_index = jnp.clip(micro_now, 0, micro_count - 1)
        if tick_back == 0:
            received = jnp.zeros_like(buffers["send_backward"])
        else:
            received = from_behind(buffers["send_backward"], "section", -1)
        upstream = jnp.where(
            segment_index == segment_count - 1,
            lax.dynamic_index_in_dim(cotangent, slot_index, 0, keepdims=False),
            received,
        )
        upstream = jnp.where(active, upstream, jnp.zeros_like(upstream))
        hidden = lax.dynamic_index_in_dim(buffers["hidden_saved"], slot_index, 0, keepdims=False)
        scaling = inverse_rms(hidden)
        normed_cols = lax.dynamic_index_in_dim(
            buffers["normed_saved"], slot_index, 0, keepdims=False
        )
        row_piece = lax.all_gather(upstream, "tensor", axis=0, tiled=True)
        weight_total = buffers["weight_total"]
        weight_total = weight_total + lax.dot_general(
            normed_cols, row_piece, (((0,), (0,)), ((), ())), preferred_element_type=jnp.float32
        )
        piece_grad = lax.dot_general(
            row_piece, weight_block, (((1,), (1,)), ((), ())), preferred_element_type=jnp.float32
        )
        grad_cols = piece_grad
        weight_total, grad_cols = (weight_total, grad_cols)
        grad_normed = lax.all_to_all(
            grad_cols.astype(jnp.bfloat16), "tensor", split_axis=0, concat_axis=1, tiled=True
        ).astype(jnp.float32)
        unrounded = hidden * scaling
        grad_hidden = upstream.astype(jnp.float32) + scaling * (
            grad_normed - unrounded * jnp.mean(grad_normed * unrounded, axis=-1, keepdims=True)
        )
        grad_sent = grad_hidden.astype(jnp.bfloat16)
        buffers["weight_total"] = weight_total
        buffers["send_backward"] = grad_sent
        buffers["grads_out"] = store_slot(buffers["grads_out"], grad_sent, slot_index, active)

    for tick_now in range(tick_count + segment_count - 1):
        if tick_now < tick_count:
            forward_tick(tick_now)
        if tick_now >= segment_count - 1:
            backward_tick(tick_now - segment_count + 1)
    weight_grad = lax.psum_scatter(
        buffers["weight_total"].astype(jnp.bfloat16), "dp", scatter_dimension=1, tiled=True
    ).astype(jnp.float32)
    return (buffers["deltas_out"][None], buffers["grads_out"][None], weight_grad[None])


def solution(mesh):
    return jax.shard_map(
        local,
        mesh=mesh,
        in_specs=(
            P(None, ("dp", "tensor"), None),
            P("section", "tensor", None),
            P("section", None, None, ("dp", "tensor"), None),
            P("section", None, None, "dp", None),
            P(None, ("dp", "tensor"), None),
        ),
        out_specs=(
            P("section", None, ("dp", "tensor"), None),
            P("section", None, ("dp", "tensor"), None),
            P("section", "tensor", "dp"),
        ),
        check_vma=False,
    )
```

profile of v0, /device:TPU:0, one launch (start us, length us, event | category | flops | bytes accessed | tf_op | source)
XLA Modules:
  0.0 1415.1 jit_solution(17899030493506179647)
XLA Ops:
  17.7 35.4 %all_to_all.285 = bf16[64,4,1024]{2,0,1:T(8,128)(2,1)S(1)} all-to-all(bf16[64,4,1024]{2,0,1:T(8,128)(2,1)S(1)} %fusion.250), channel_id=1, replica_groups=mesh['dp'=4,'section'=2,'tensor'=4] {'tensor'}, dimensions={1} | all-to-all | bytes 1048576 | tf_op jit(solution)/shard_map/all_to_all | solution.py:80
  80.5 42.9 %reduce-scatter.11.cloned.1.call-done = bf16[64,4096]{1,0:T(8,128)(2,1)} async-done(((bf16[256,4096]{1,0:T(8,128)(2,1)}), bf16[64,4096]{1,0:T(8,128)(2,1)}) %reduce-scatter.11.cloned.1.call-update) | async-done | bytes 524304 | tf_op jit(solution)/shard_map/reduce_scatter | solution.py:81
  125.8 11.8 pmax.63
  169.0 29.2 %all_to_all.286 = bf16[64,4,1024]{2,0,1:T(8,128)(2,1)S(1)} all-to-all(bf16[64,4,1024]{2,0,1:T(8,128)(2,1)S(1)} %bitcast.990), channel_id=1, replica_groups=mesh['dp'=4,'section'=2,'tensor'=4] {'tensor'}, dimensions={1} | all-to-all | bytes 1048576 | tf_op jit(solution)/shard_map/all_to_all | solution.py:80
  231.4 43.1 %reduce-scatter.13.cloned.1.call-done = bf16[64,4096]{1,0:T(8,128)(2,1)} async-done(((bf16[256,4096]{1,0:T(8,128)(2,1)}), bf16[64,4096]{1,0:T(8,128)(2,1)}) %reduce-scatter.13.cloned.1.call-update) | async-done | bytes 524304 | tf_op jit(solution)/shard_map/reduce_scatter | solution.py:81
  276.2 11.8 pmax.64
  319.2 29.3 %all_to_all.287 = bf16[64,4,1024]{2,0,1:T(8,128)(2,1)S(1)} all-to-all(bf16[64,4,1024]{2,0,1:T(8,128)(2,1)S(1)} %bitcast.992), channel_id=1, replica_groups=mesh['dp'=4,'section'=2,'tensor'=4] {'tensor'}, dimensions={1} | all-to-all | bytes 1048576 | tf_op jit(solution)/shard_map/all_to_all | solution.py:80
  356.4 14.5 %all-gather.13.cloned.1.call-done = bf16[256,4096]{1,0:T(8,128)(2,1)} async-done(((bf16[64,4096]{1,0:T(8,128)(2,1)}), bf16[256,4096]{1,0:T(8,128)(2,1)}) %all-gather.13.cloned.1.call-update) | async-done | bytes 2097168 | tf_op jit(solution)/shard_map/all_gather | solution.py:122
  381.6 43.1 %reduce-scatter.15.cloned.1.call-done = bf16[64,4096]{1,0:T(8,128)(2,1)} async-done(((bf16[256,4096]{1,0:T(8,128)(2,1)}), bf16[64,4096]{1,0:T(8,128)(2,1)}) %reduce-scatter.15.cloned.1.call-update) | async-done | bytes 524304 | tf_op jit(solution)/shard_map/reduce_scatter | solution.py:81
  426.5 11.8 pmax.65
  463.9 29.3 %all_to_all.288 = bf16[64,4,1024]{2,0,1:T(8,128)(2,1)S(1)} all-to-all(bf16[64,4,1024]{2,0,1:T(8,128)(2,1)S(1)} %bitcast.994), channel_id=1, replica_groups=mesh['dp'=4,'section'=2,'tensor'=4] {'tensor'}, dimensions={1} | all-to-all | bytes 1048576 | tf_op jit(solution)/shard_map/all_to_all | solution.py:80
  501.1 14.5 %all-gather.15.cloned.1.call-done = bf16[256,4096]{1,0:T(8,128)(2,1)} async-done(((bf16[64,4096]{1,0:T(8,128)(2,1)}), bf16[256,4096]{1,0:T(8,128)(2,1)}) %all-gather.15.cloned.1.call-update) | async-done | bytes 2097168 | tf_op jit(solution)/shard_map/all_gather | solution.py:122
  526.4 43.2 %reduce-scatter.17.cloned.1.call-done = bf16[64,4096]{1,0:T(8,128)(2,1)} async-done(((bf16[256,4096]{1,0:T(8,128)(2,1)}), bf16[64,4096]{1,0:T(8,128)(2,1)}) %reduce-scatter.17.cloned.1.call-update) | async-done | bytes 524304 | tf_op jit(solution)/shard_map/reduce_scatter | solution.py:81
  571.3 11.8 pmax.66
  609.2 29.5 %all_to_all.289 = bf16[64,4,1024]{2,0,1:T(8,128)(2,1)S(1)} all-to-all(bf16[64,4,1024]{2,0,1:T(8,128)(2,1)S(1)} %bitcast.996), channel_id=1, replica_groups=mesh['dp'=4,'section'=2,'tensor'=4] {'tensor'}, dimensions={1} | all-to-all | bytes 1048576 | tf_op jit(solution)/shard_map/all_to_all | solution.py:80
  646.7 14.2 %all-gather.17.cloned.1.call-done = bf16[256,4096]{1,0:T(8,128)(2,1)} async-done(((bf16[64,4096]{1,0:T(8,128)(2,1)}), bf16[256,4096]{1,0:T(8,128)(2,1)}) %all-gather.17.cloned.1.call-update) | async-done | bytes 2097168 | tf_op jit(solution)/shard_map/all_gather | solution.py:122
  671.6 43.1 %reduce-scatter.19.cloned.1.call-done = bf16[64,4096]{1,0:T(8,128)(2,1)} async-done(((bf16[256,4096]{1,0:T(8,128)(2,1)}), bf16[64,4096]{1,0:T(8,128)(2,1)}) %reduce-scatter.19.cloned.1.call-update) | async-done | bytes 524304 | tf_op jit(solution)/shard_map/reduce_scatter | solution.py:81
  716.4 11.8 pmax.67
  753.9 29.6 %all_to_all.290 = bf16[64,4,1024]{2,0,1:T(8,128)(2,1)S(1)} all-to-all(bf16[64,4,1024]{2,0,1:T(8,128)(2,1)S(1)} %bitcast.998), channel_id=1, replica_groups=mesh['dp'=4,'section'=2,'tensor'=4] {'tensor'}, dimensions={1} | all-to-all | bytes 1048576 | tf_op jit(solution)/shard_map/all_to_all | solution.py:80
  791.4 14.4 %all-gather.19.cloned.1.call-done = bf16[256,4096]{1,0:T(8,128)(2,1)} async-done(((bf16[64,4096]{1,0:T(8,128)(2,1)}), bf16[256,4096]{1,0:T(8,128)(2,1)}) %all-gather.19.cloned.1.call-update) | async-done | bytes 2097168 | tf_op jit(solution)/shard_map/all_gather | solution.py:122
  816.5 43.0 %reduce-scatter.21.cloned.1.call-done = bf16[64,4096]{1,0:T(8,128)(2,1)} async-done(((bf16[256,4096]{1,0:T(8,128)(2,1)}), bf16[64,4096]{1,0:T(8,128)(2,1)}) %reduce-scatter.21.cloned.1.call-update) | async-done | bytes 524304 | tf_op jit(solution)/shard_map/reduce_scatter | solution.py:81
  861.3 11.8 pmax.68
  898.7 29.6 %all_to_all.291 = bf16[64,4,1024]{2,0,1:T(8,128)(2,1)S(1)} all-to-all(bf16[64,4,1024]{2,0,1:T(8,128)(2,1)S(1)} %bitcast.1000), channel_id=1, replica_groups=mesh['dp'=4,'section'=2,'tensor'=4] {'tensor'}, dimensions={1} | all-to-all | bytes 1048576 | tf_op jit(solution)/shard_map/all_to_all | solution.py:80
  936.3 14.3 %all-gather.21.cloned.1.call-done = bf16[256,4096]{1,0:T(8,128)(2,1)} async-done(((bf16[64,4096]{1,0:T(8,128)(2,1)}), bf16[256,4096]{1,0:T(8,128)(2,1)}) %all-gather.21.cloned.1.call-update) | async-done | bytes 2097168 | tf_op jit(solution)/shard_map/all_gather | solution.py:122
  961.4 43.0 %reduce-scatter.23.cloned.1.call-done = bf16[64,4096]{1,0:T(8,128)(2,1)} async-done(((bf16[256,4096]{1,0:T(8,128)(2,1)}), bf16[64,4096]{1,0:T(8,128)(2,1)}) %reduce-scatter.23.cloned.1.call-update) | async-done | bytes 524304 | tf_op jit(solution)/shard_map/reduce_scatter | solution.py:81
  1006.1 11.8 pmax.69
  1048.4 28.5 %all-to-all-done.7 = bf16[64,4,1024]{2,0,1:T(8,128)(2,1)S(1)} async-done(((bf16[64,4,1024]{2,0,1:T(8,128)(2,1)}), bf16[64,4,1024]{2,0,1:T(8,128)(2,1)S(1)}, u32[]{:S(2)}, u32[]{:S(2)}) %all-to-all-start.7) | async-done | bytes 524320 | tf_op jit(solution)/shard_map/all_to_all | solution.py:80
  1134.7 12.9 reduce-scatter.25.cloned.1.call-done
  1149.3 11.7 pmax.70
  1234.2 18.1 %all-to-all-done.8 = bf16[64,4,1024]{2,0,1:T(8,128)(2,1)S(1)} async-done(((bf16[64,4,1024]{2,0,1:T(8,128)(2,1)}), bf16[64,4,1024]{2,0,1:T(8,128)(2,1)S(1)}, u32[]{:S(2)}, u32[]{:S(2)}) %all-to-all-start.8) | async-done | bytes 524320 | tf_op jit(solution)/shard_map/all_to_all | solution.py:80
  1272.0 46.0 %add_convert_fusion = bf16[1024,4096]{1,0:T(8,128)(2,1)} fusion(f32[1024,4096]{1,0:T(8,128)} %fusion.262, f32[1024,4096]{1,0:T(8,128)} %fusion.264, f32[1024,4096]{1,0:T(8,128)} %fusion.266, f32[1024,4096]{1,0:T(8,128)} %fusion.268, f32[1024,4096]{1,0:T(8,128)} %fusion.270, f32[1024,4096]{1,0:T(8,128)} %fusion.272, f32[1024,4096]{1,0:T(8,128)} %fusion.63, ...), kind=kOutput, calls=%fused_computation | convolution fusion | flops 2185232384 | bytes 145227776 | tf_op jit(solution)/shard_map/dot_general | solution.py:124
  1365.4 38.6 %reduce-scatter.29.cloned.1.call-done = bf16[1024,1024]{1,0:T(8,128)(2,1)} async-done(((bf16[1024,4096]{1,0:T(8,128)(2,1)}), bf16[1024,1024]{1,0:T(8,128)(2,1)}) %reduce-scatter.29.cloned.1.call-update) | async-done | bytes 2097168 | tf_op jit(solution)/shard_map/reduce_scatter | solution.py:149
  (405 shorter events, 575.7 us)
Async XLA Ops:
  7.2 62.6 %all-gather.27.cloned.1.call-start = ((), (), s32[]{:S(2)}) async-start(), calls=%async_computation.46 | async-start | bytes 2621440 | tf_op jit(solution)/shard_map/all_gather | solution.py:122
  9.1 114.3 %reduce-scatter.11.cloned.1.call-start = ((), (), s32[]{:S(2)}) async-start(), calls=%async_computation.28 | async-start | bytes 2621440 | tf_op jit(solution)/shard_map/reduce_scatter | solution.py:81
  76.9 73.8 %all-to-all-start.9 = ((bf16[4,64,1024]{2,1,0:T(8,128)(2,1)}), bf16[4,64,1024]{2,1,0:T(8,128)(2,1)S(1)}, u32[]{:S(2)}, u32[]{:S(2)}) async-start(bf16[4,64,1024]{2,1,0:T(8,128)(2,1)} %bitcast.115), calls=%async_computation.18 | async-start | bytes 1048576 | tf_op jit(solution)/shard_map/all_to_all | solution.py:132
  80.4 140.3 %all-gather.11.cloned.1.call-start = ((), (), s32[]{:S(2)}) async-start(), calls=%async_computation.37 | async-start | bytes 2621440 | tf_op jit(solution)/shard_map/all_gather | solution.py:122
  168.6 105.9 %reduce-scatter.13.cloned.1.call-start = ((), (), s32[]{:S(2)}) async-start(), calls=%async_computation.29 | async-start | bytes 2621440 | tf_op jit(solution)/shard_map/reduce_scatter | solution.py:81
  227.9 73.1 %all-to-all-start.10 = ((bf16[4,64,1024]{2,1,0:T(8,128)(2,1)}), bf16[4,64,1024]{2,1,0:T(8,128)(2,1)S(1)}, u32[]{:S(2)}, u32[]{:S(2)}) async-start(bf16[4,64,1024]{2,1,0:T(8,128)(2,1)} %bitcast.121), calls=%async_computation.19 | async-start | bytes 1048576 | tf_op jit(solution)/shard_map/all_to_all | solution.py:132
  231.4 139.6 %all-gather.13.cloned.1.call-start = ((), (), s32[]{:S(2)}) async-start(), calls=%async_computation.38 | async-start | bytes 2621440 | tf_op jit(solution)/shard_map/all_gather | solution.py:122
  318.8 105.9 %reduce-scatter.15.cloned.1.call-start = ((), (), s32[]{:S(2)}) async-start(), calls=%async_computation.30 | async-start | bytes 2621440 | tf_op jit(solution)/shard_map/reduce_scatter | solution.py:81
  378.1 67.7 %all-to-all-start.11 = ((bf16[4,64,1024]{2,1,0:T(8,128)(2,1)}), bf16[4,64,1024]{2,1,0:T(8,128)(2,1)S(1)}, u32[]{:S(2)}, u32[]{:S(2)}) async-start(bf16[4,64,1024]{2,1,0:T(8,128)(2,1)} %bitcast.127), calls=%async_computation.20 | async-start | bytes 1048576 | tf_op jit(solution)/shard_map/all_to_all | solution.py:132
  381.6 134.1 %all-gather.15.cloned.1.call-start = ((), (), s32[]{:S(2)}) async-start(), calls=%async_computation.39 | async-start | bytes 2621440 | tf_op jit(solution)/shard_map/all_gather | solution.py:122
  463.5 106.1 %reduce-scatter.17.cloned.1.call-start = ((), (), s32[]{:S(2)}) async-start(), calls=%async_computation.31 | async-start | bytes 2621440 | tf_op jit(solution)/shard_map/reduce_scatter | solution.py:81
  522.8 67.6 %all-to-all-start.12 = ((bf16[4,64,1024]{2,1,0:T(8,128)(2,1)}), bf16[4,64,1024]{2,1,0:T(8,128)(2,1)S(1)}, u32[]{:S(2)}, u32[]{:S(2)}) async-start(bf16[4,64,1024]{2,1,0:T(8,128)(2,1)} %bitcast.133), calls=%async_computation.21 | async-start | bytes 1048576 | tf_op jit(solution)/shard_map/all_to_all | solution.py:132
  526.3 134.6 %all-gather.17.cloned.1.call-start = ((), (), s32[]{:S(2)}) async-start(), calls=%async_computation.40 | async-start | bytes 2621440 | tf_op jit(solution)/shard_map/all_gather | solution.py:122
  608.3 106.3 %reduce-scatter.19.cloned.1.call-start = ((), (), s32[]{:S(2)}) async-start(), calls=%async_computation.32 | async-start | bytes 2621440 | tf_op jit(solution)/shard_map/reduce_scatter | solution.py:81
  668.1 67.5 %all-to-all-start.13 = ((bf16[4,64,1024]{2,1,0:T(8,128)(2,1)}), bf16[4,64,1024]{2,1,0:T(8,128)(2,1)S(1)}, u32[]{:S(2)}, u32[]{:S(2)}) async-start(bf16[4,64,1024]{2,1,0:T(8,128)(2,1)} %bitcast.139), calls=%async_computation.22 | async-start | bytes 1048576 | tf_op jit(solution)/shard_map/all_to_all | solution.py:132
  671.5 134.2 %all-gather.19.cloned.1.call-start = ((), (), s32[]{:S(2)}) async-start(), calls=%async_computation.41 | async-start | bytes 2621440 | tf_op jit(solution)/shard_map/all_gather | solution.py:122
  753.4 106.1 %reduce-scatter.21.cloned.1.call-start = ((), (), s32[]{:S(2)}) async-start(), calls=%async_computation.33 | async-start | bytes 2621440 | tf_op jit(solution)/shard_map/reduce_scatter | solution.py:81
  813.0 67.4 %all-to-all-start.14 = ((bf16[4,64,1024]{2,1,0:T(8,128)(2,1)}), bf16[4,64,1024]{2,1,0:T(8,128)(2,1)S(1)}, u32[]{:S(2)}, u32[]{:S(2)}) async-start(bf16[4,64,1024]{2,1,0:T(8,128)(2,1)} %bitcast.145), calls=%async_computation.23 | async-start | bytes 1048576 | tf_op jit(solution)/shard_map/all_to_all | solution.py:132
  816.4 134.2 %all-gather.21.cloned.1.call-start = ((), (), s32[]{:S(2)}) async-start(), calls=%async_computation.42 | async-start | bytes 2621440 | tf_op jit(solution)/shard_map/all_gather | solution.py:122
  898.3 106.1 %reduce-scatter.23.cloned.1.call-start = ((), (), s32[]{:S(2)}) async-start(), calls=%async_computation.34 | async-start | bytes 2621440 | tf_op jit(solution)/shard_map/reduce_scatter | solution.py:81
  957.8 67.4 %all-to-all-start.15 = ((bf16[4,64,1024]{2,1,0:T(8,128)(2,1)}), bf16[4,64,1024]{2,1,0:T(8,128)(2,1)S(1)}, u32[]{:S(2)}, u32[]{:S(2)}) async-start(bf16[4,64,1024]{2,1,0:T(8,128)(2,1)} %bitcast.151), calls=%async_computation.24 | async-start | bytes 1048576 | tf_op jit(solution)/shard_map/all_to_all | solution.py:132
  961.3 162.4 %all-gather.23.cloned.1.call-start = ((), (), s32[]{:S(2)}) async-start(), calls=%async_computation.43 | async-start | bytes 2621440 | tf_op jit(solution)/shard_map/all_gather | solution.py:122
  1044.3 32.6 %all-to-all-start.7 = ((bf16[64,4,1024]{2,0,1:T(8,128)(2,1)}), bf16[64,4,1024]{2,0,1:T(8,128)(2,1)S(1)}, u32[]{:S(2)}, u32[]{:S(2)}) async-start(bf16[64,4,1024]{2,0,1:T(8,128)(2,1)} %bitcast.969), calls=%async_computation.14 | async-start | bytes 1048576 | tf_op jit(solution)/shard_map/all_to_all | solution.py:80
  1047.8 99.8 %reduce-scatter.25.cloned.1.call-start = ((), (), s32[]{:S(2)}) async-start(), calls=%async_computation.35 | async-start | bytes 2621440 | tf_op jit(solution)/shard_map/reduce_scatter | solution.py:81
  1131.2 48.5 %all-to-all-start.16 = ((bf16[4,64,1024]{2,1,0:T(8,128)(2,1)}), bf16[4,64,1024]{2,1,0:T(8,128)(2,1)S(1)}, u32[]{:S(2)}, u32[]{:S(2)}) async-start(bf16[4,64,1024]{2,1,0:T(8,128)(2,1)} %bitcast.157), calls=%async_computation.25 | async-start | bytes 1048576 | tf_op jit(solution)/shard_map/all_to_all | solution.py:132
  1134.6 137.3 %all-gather.25.cloned.1.call-start = ((), (), s32[]{:S(2)}) async-start(), calls=%async_computation.44 | async-start | bytes 2621440 | tf_op jit(solution)/shard_map/all_gather | solution.py:122
  1167.0 13.9 collective-permute-start.7
  1192.5 12.9 collective-permute-start.15
  1218.8 33.6 %all-to-all-start.8 = ((bf16[64,4,1024]{2,0,1:T(8,128)(2,1)}), bf16[64,4,1024]{2,0,1:T(8,128)(2,1)S(1)}, u32[]{:S(2)}, u32[]{:S(2)}) async-start(bf16[64,4,1024]{2,0,1:T(8,128)(2,1)} %bitcast.968), calls=%async_computation.16 | async-start | bytes 1048576 | tf_op jit(solution)/shard_map/all_to_all | solution.py:80
  1222.3 125.6 %reduce-scatter.27.cloned.1.call-start = ((), (), s32[]{:S(2)}) async-start(), calls=%async_computation.36 | async-start | bytes 2621440 | tf_op jit(solution)/shard_map/reduce_scatter | solution.py:81
  1259.5 144.5 %reduce-scatter.29.cloned.1.call-start = ((), (), s32[]{:S(2)}) async-start(), calls=%async_computation.45 | async-start | bytes 10485760 | tf_op jit(solution)/shard_map/reduce_scatter | solution.py:149
  1325.1 18.5 %all-to-all-start.17 = ((bf16[4,64,1024]{2,1,0:T(8,128)(2,1)}), bf16[4,64,1024]{2,1,0:T(8,128)(2,1)S(1)}, u32[]{:S(2)}, u32[]{:S(2)}) async-start(bf16[4,64,1024]{2,1,0:T(8,128)(2,1)} %bitcast.163), calls=%async_computation.26 | async-start | bytes 1048576 | tf_op jit(solution)/shard_map/all_to_all | solution.py:132
  (48 other events, 256.5 us)
Sparse Core Ops, SparseCore 0:
  10.1 59.6 all-gather.26
  72.6 50.7 reduce-scatter.10
  168.7 52.0 all-gather.10
  223.4 51.0 reduce-scatter.12
  318.9 52.0 all-gather.12
  373.7 51.0 reduce-scatter.14
  463.6 52.0 all-gather.14
  518.5 51.0 reduce-scatter.16
  608.4 52.3 all-gather.16
  663.6 51.0 reduce-scatter.18
  753.6 52.1 all-gather.18
  808.5 50.9 reduce-scatter.20
  898.4 52.2 all-gather.20
  953.4 50.9 reduce-scatter.22
  1043.3 53.8 all-gather.22
  1099.9 47.6 reduce-scatter.24
  1207.5 55.7 all-gather.24
  1265.5 42.3 reduce-scatter.26
  1318.1 85.9 reduce-scatter.28
where the time goes:
time: 1430 us; the launch traced here: 1420 us
  waiting for transfers between devices  512 us (36%)
  blocking collectives  316 us (22%)
  matrix products  251 us (18%)
  other arithmetic  195 us (14%)
  starting transfers between devices  62.9 us (4%)
  local copies, waits for them, and re-layouts  62.3 us (4%)
  between operations  15.4 us (1%)
    reduce_scatter x9, waiting for transfers between devices, forward_tick(): lax.psum_scatter(jnp.dot(normed_cols, weight_block, preferred_element_typ...  314 us
    all_to_all x7, blocking collectives, forward_tick(): lax.all_to_all(normed, 'tensor', split_axis=1, concat_axis=0, tiled=True)  212 us
    dot_general x9, matrix products, backward_tick(): lax.dot_general(normed_cols, row_piece, (((0,), (0,)), ((), ())), preferr...  122 us
    select_n x36, other arithmetic, store_slot(): return jnp.where(active, updated, buffer)  116 us
    pmax x9, blocking collectives, forward_tick(): merged = lax.pmax(local_peak, 'tensor') + epsilon  104 us
    all_gather x9, waiting for transfers between devices, backward_tick(): row_piece = lax.all_gather(upstream, 'tensor', axis=0, tiled=True)  90.5 us
    dot_general x9, matrix products, backward_tick(): lax.dot_general(row_piece, weight_block, (((1,), (1,)), ((), ())), prefer...  64.8 us
    dot_general x9, matrix products, forward_tick(): jnp.dot(normed_cols, weight_block, preferred_element_type=jnp.float32)  64 us
  transfers between devices with their start and end apart: 46, of which 30 were waited for; matrix products, arithmetic and copies ran while one was open for 28% of the time, Pallas kernels for 0%

commit v1 on v0

v1 whole, which is shorter than its diff:
```python
import jax
import jax.numpy as jnp
from jax import lax
from jax.sharding import PartitionSpec as P

code_levels = 7.0
softness = 0.8
two_pi = 6.283185307179586
epsilon = 1e-06
bf16 = jnp.bfloat16
f32 = jnp.float32
chunk_count = 1

sine_terms = (
    6.283185307179586, -41.34170224039975, 81.60524927607504, -76.70585975306136,
    42.058693944897654, -15.094642576822985, 3.8199525848482821,
)


def sine_of_turns(turns):
    rest = turns - jnp.round(turns)
    rest = jnp.where(rest > 0.25, 0.5 - rest, jnp.where(rest < -0.25, -0.5 - rest, rest))
    square = rest * rest
    total = jnp.full_like(rest, sine_terms[-1])
    for term in sine_terms[-2::-1]:
        total = total * square + term
    return total * rest


def local(in_delta, weight, cache_codes, cache_scales, cotangent):
    dp_count = lax.axis_size("dp")
    section_count = lax.axis_size("section")
    replica = lax.axis_index("dp")
    first = lax.axis_index("section") == 0
    micro_count, rows, width = in_delta.shape
    block_count = cache_scales.shape[-1]
    block = width // block_count
    part = width // dp_count
    is_power = dp_count & (dp_count - 1) == 0
    chunks = chunk_count if micro_count % chunk_count == 0 else 1
    micros = micro_count // chunks
    tokens = micros * rows

    def target(source, step):
        return source ^ step if is_power else (source + step) % dp_count

    def origin(source, step):
        return source ^ step if is_power else (source - step) % dp_count

    def exchange(value, section, step):
        pairs = [
            (source * section_count + section, target(source, step) * section_count + section)
            for source in range(dp_count)
        ]
        return lax.ppermute(value, ("dp", "section"), pairs)

    def give_back(value, section, step):
        pairs = [
            (source * section_count + section, origin(source, step) * section_count + section)
            for source in range(dp_count)
        ]
        return lax.ppermute(value, ("dp", "section"), pairs)

    def columns(value, index):
        return lax.dynamic_slice_in_dim(value, index * part, part, 1)

    weight_part = lax.all_gather(columns(weight[0], replica), "tensor", axis=0, tiled=True)

    def product(forward_here, whole, piece):
        def forward(whole, piece):
            out = jnp.dot(whole, weight_part, preferred_element_type=f32).astype(bf16)
            return out, jnp.zeros((tokens, width), bf16)

        def backward(whole, piece):
            out = lax.dot_general(
                piece, weight_part, (((1,), (1,)), ((), ())), preferred_element_type=f32
            ).astype(bf16)
            return jnp.zeros((tokens, part), bf16), out

        return lax.cond(forward_here, forward, backward, whole, piece)

    def pre(normed, upstream, forward_section):
        whole, piece = [normed], [columns(upstream, replica)]
        for step in range(1, dp_count):
            whole.append(exchange(normed, forward_section, step))
            piece.append(
                exchange(columns(upstream, target(replica, step)), 1 - forward_section, step)
            )
        return whole, piece

    def middle(whole, piece, forward_section):
        here = first if forward_section == 0 else ~first
        branch = jnp.zeros((tokens, width), bf16)
        grad = None
        order = list(range(1, dp_count)) + [0]
        for step in order:
            out, back = product(here, whole[step], piece[step])
            if step:
                out = give_back(out, forward_section, step)
                back = give_back(back, 1 - forward_section, step)
            branch = lax.dynamic_update_slice_in_dim(
                branch, out, target(replica, step) * part, 1
            )
            grad = back.astype(f32) if grad is None else grad + back.astype(f32)
        return branch, grad

    def scales_row(slot, chunk):
        now = cache_scales[0, slot, chunk * micros:(chunk + 1) * micros, 0]
        return jnp.repeat(now / code_levels, block, axis=-1)[:, None, :]

    def codes(slot, chunk):
        return cache_codes[0, slot, chunk * micros:(chunk + 1) * micros].astype(f32)

    def shaped(value):
        return value.reshape(micros, rows, width)

    def flat(value):
        return value.reshape(tokens, width)

    def rms(hidden):
        return lax.rsqrt(jnp.mean(hidden * hidden, axis=-1, keepdims=True) + epsilon)

    def finish_forward(hidden, branch, chunk):
        delta = hidden + shaped(branch).astype(f32) - codes(1, chunk) * scales_row(1, chunk)
        peak = jnp.max(jnp.abs(delta), axis=1).reshape(micros, block_count, block).max(axis=-1)
        spread = lax.pmax(peak, "tensor") + epsilon
        up_scale = jnp.repeat(code_levels / spread, block, axis=-1)[:, None, :]
        down_scale = jnp.repeat(spread / code_levels, block, axis=-1)[:, None, :]
        level = delta * up_scale
        smooth = level - (softness / two_pi) * sine_of_turns(level)
        return (smooth * down_scale).astype(bf16)

    def finish_backward(hidden, upstream, grad):
        inverse = rms(hidden)
        grad = shaped(grad.astype(bf16)).astype(f32)
        unrounded = hidden * inverse
        mean = jnp.mean(grad * unrounded, axis=-1, keepdims=True)
        return (upstream.astype(f32) + inverse * (grad - unrounded * mean)).astype(bf16)

    over = range(chunks)
    span = [slice(c * micros, (c + 1) * micros) for c in over]
    outs, grads, wholes, pieces = [None] * chunks, [None] * chunks, [], []

    with jax.named_scope("phase_a"):
        stage_a = []
        for c in over:
            hidden = codes(0, c) * scales_row(0, c) + in_delta[span[c]].astype(f32)
            normed = flat((hidden * rms(hidden)).astype(bf16))
            stage_a.append((hidden, pre(normed, flat(cotangent[span[c]]), 0)))
        stage_b = []
        for c in over:
            hidden, (whole, piece) = stage_a[c]
            branch, grad = middle(whole, piece, 0)
            outs[c] = finish_forward(hidden, branch, c)
            received = lax.ppermute(outs[c], "section", [(0, 1)])
            incoming = jnp.where(first, in_delta[span[c]], received)
            hidden = codes(0, c) * scales_row(0, c) + incoming.astype(f32)
            normed = flat((hidden * rms(hidden)).astype(bf16))
            grads[c] = finish_backward(hidden, cotangent[span[c]], grad)
            upstream = lax.ppermute(grads[c], "section", [(1, 0)])
            stage_b.append((hidden, upstream, pre(normed, flat(upstream), 1)))

    with jax.named_scope("weight_grad"):
        def gathered(pairs):
            whole = jnp.concatenate([w for p in pairs for w in p[0]], axis=0)
            piece = jnp.concatenate([g for p in pairs for g in p[1]], axis=0)
            return lax.dot_general(
                whole, piece, (((0,), (0,)), ((), ())), preferred_element_type=f32
            ).astype(bf16)

        from_a = [a[1] for a in stage_a]
        from_b = [b[2] for b in stage_b]
        partial = lax.cond(
            first,
            lambda a, b: gathered([(x[0], y[1]) for x, y in zip(a, b)]),
            lambda a, b: gathered([(y[0], x[1]) for x, y in zip(a, b)]),
            from_a,
            from_b,
        )
        weight_grad = lax.psum_scatter(
            partial, "tensor", scatter_dimension=0, tiled=True
        ).astype(f32)

    with jax.named_scope("phase_b"):
        for c in over:
            hidden, upstream, (whole, piece) = stage_b[c]
            branch, grad = middle(whole, piece, 1)
            outs[c] = jnp.where(first, outs[c], finish_forward(hidden, branch, c))
            grads[c] = jnp.where(first, finish_backward(hidden, upstream, grad), grads[c])

    def joined(values):
        return values[0] if chunks == 1 else jnp.concatenate(values, axis=0)

    return (joined(outs)[None], joined(grads)[None], weight_grad[None])


def solution(mesh):
    return jax.shard_map(
        local,
        mesh=mesh,
        in_specs=(
            P(None, ("dp", "tensor"), None),
            P("section", "tensor", None),
            P("section", None, None, ("dp", "tensor"), None),
            P("section", None, None, "dp", None),
            P(None, ("dp", "tensor"), None),
        ),
        out_specs=(
            P("section", None, ("dp", "tensor"), None),
            P("section", None, ("dp", "tensor"), None),
            P("section", "tensor", "dp"),
        ),
        check_vma=False,
    )
```

time: 1430 us -> 660 us (0.46)
  blocking collectives: 316 us -> 33.9 us
  waiting for transfers between devices: 512 us -> 299 us
  matrix products: 251 us -> 104 us
  other arithmetic: 195 us -> 101 us
  local copies, waits for them, and re-layouts: 62.3 us -> 29.3 us
    reduce_scatter x10 -> x1, waiting for transfers between devices: 353 us -> 25.2 us  [local(): lax.psum_scatter(partial, 'tensor', scatter_dimension=0, tiled=True)]
    all_to_all x7 -> x0, blocking collectives: 212 us -> none  [forward_tick(): lax.all_to_all(normed, 'tensor', split_axis=1, concat_axis=0, tiled=True)]
    dot_general x27 -> x9, matrix products: 251 us -> 104 us  [the longest x4 40.9 us: backward(): lax.dot_general(piece, weight_part, (((1,), (1,)), ((), ())), preferred_e...]
    ppermute x16 -> x26, waiting for transfers between devices: 18.4 us -> 154 us  [the longest x12 77.2 us: give_back(): return lax.ppermute(value, ('dp', 'section'), pairs)]
    select_n x45 -> x0, other arithmetic: 133 us -> none  [the longest x36 116 us: store_slot(): return jnp.where(active, updated, buffer)]
    pmax x9 -> x2, blocking collectives: 104 us -> 33.9 us  [finish_forward(): spread = lax.pmax(peak, 'tensor') + epsilon]
    all_to_all x11 -> x0, waiting for transfers between devices: 50.2 us -> none  [the longest x2 46.6 us: forward_tick(): lax.all_to_all(normed, 'tensor', split_axis=1, concat_axis=0, tiled=True)]
    ppermute x16 -> x26, starting transfers between devices: 22.8 us -> 65.5 us  [the longest x12 32.1 us: exchange(): return lax.ppermute(value, ('dp', 'section'), pairs)]
  transfers between devices with their start and end apart: 46 -> 28, of which waited for: 30 -> 9; matrix products, arithmetic and copies ran while one was open for 28% -> 28% of each run, Pallas kernels for 0% -> 0%
where the time goes in v1:
time: 660 us; the launch traced here: 651 us
  waiting for transfers between devices  299 us (45%)
  matrix products  104 us (16%)
  other arithmetic  101 us (15%)
  starting transfers between devices  65.6 us (10%)
  blocking collectives  33.9 us (5%)
  local copies, waits for them, and re-layouts  29.3 us (4%)
  between operations  15.3 us (2%)
    all_gather x1, waiting for transfers between devices, local(): lax.all_gather(columns(weight[0], replica), 'tensor', axis=0, tiled=True)  120 us
    ppermute x12, waiting for transfers between devices, give_back(): return lax.ppermute(value, ('dp', 'section'), pairs)  77.2 us
    ppermute x12, waiting for transfers between devices, exchange(): return lax.ppermute(value, ('dp', 'section'), pairs)  42.2 us
    dot_general x4, matrix products, backward(): lax.dot_general(piece, weight_part, (((1,), (1,)), ((), ())), preferred_e...  40.9 us
    dot_general x4, matrix products, forward(): out = jnp.dot(whole, weight_part, preferred_element_type=f32).astype(bf16)  39.7 us
    ppermute x1, waiting for transfers between devices, local(): upstream = lax.ppermute(grads[c], 'section', [(1, 0)])  34.6 us
    pmax x2, blocking collectives, finish_forward(): spread = lax.pmax(peak, 'tensor') + epsilon  33.9 us
    ppermute x12, starting transfers between devices, exchange(): return lax.ppermute(value, ('dp', 'section'), pairs)  32.1 us
  transfers between devices with their start and end apart: 28, of which 9 were waited for; matrix products, arithmetic and copies ran while one was open for 28% of the time, Pallas kernels for 0%

profile of v1, /device:TPU:0, one launch (start us, length us, event | category | flops | bytes accessed | tf_op | source)
XLA Modules:
  0.0 650.8 jit_solution(17518955438547281373)
XLA Ops:
  42.7 120.1 %all-gather.3.cloned.1.call-done = bf16[1,4096,1024]{2,1,0:T(8,128)(2,1)} async-done(((bf16[1,1024,1024]{2,1,0:T(8,128)(2,1)}), bf16[1,4096,1024]{2,1,0:T(8,128)(2,1)}) %all-gather.3.cloned.1.call-update) | async-done | bytes 8388624 | tf_op jit(solution)/shard_map/all_gather | solution.py:67
  162.8 10.8 %conditional.13 = (bf16[512,1024]{1,0:T(8,128)(2,1)}, bf16[512,4096]{1,0:T(8,128)(2,1)S(1)}) conditional(s32[]{:T(128)} %convert_element_type.174, (bf16[512,1024]{1,0:T(8,128)(2,1)}, bf16[4096,1024]{1,0:T(8,128)(2,1)}) %tuple.157, (bf16[512,4096]{1,0:T(8,128)(2,1)}, bf16[4096,1024]{1,0:T(8,128)(2,1)}) %tuple.142), branch_computations={%region_1.0_spmd, %region_2.0_spmd} | conditional | flops 4297064448 | bytes 17825810 | solution.py:80
  162.8 10.3 %convolution_convert_fusion.1 = bf16[512,1024]{1,0:T(8,128)(2,1)} fusion(bf16[512,4096]{1,0:T(8,128)(2,1)} %get-tuple-element.105, bf16[4096,1024]{1,0:T(8,128)(2,1)} %get-tuple-element.106), kind=kOutput, calls=%fused_computation.1 | convolution fusion | flops 4295491584 | bytes 13631488 | tf_op jit(solution)/shard_map/phase_a/cond/branch_1_fun/dot_general | solution.py:71
  177.1 10.9 %conditional.14 = (bf16[512,1024]{1,0:T(8,128)(2,1)}, bf16[512,4096]{1,0:T(8,128)(2,1)S(1)}) conditional(s32[]{:T(128)} %convert_element_type.174, (bf16[512,1024]{1,0:T(8,128)(2,1)}, bf16[4096,1024]{1,0:T(8,128)(2,1)}) %tuple.143, (bf16[512,4096]{1,0:T(8,128)(2,1)}, bf16[4096,1024]{1,0:T(8,128)(2,1)}) %tuple.144), branch_computations={%region_3.0_spmd, %region_4.0_spmd} | conditional | flops 4297064448 | bytes 17825810 | solution.py:80
  177.3 10.1 %convolution_convert_fusion.3 = bf16[512,1024]{1,0:T(8,128)(2,1)} fusion(bf16[512,4096]{1,0:T(8,128)(2,1)} %get-tuple-element.109, bf16[4096,1024]{1,0:T(8,128)(2,1)} %get-tuple-element.110), kind=kOutput, calls=%fused_computation.3 | convolution fusion | flops 4295491584 | bytes 13631488 | tf_op jit(solution)/shard_map/phase_a/cond/branch_1_fun/dot_general | solution.py:71
  191.4 11.1 %conditional.15 = (bf16[512,1024]{1,0:T(8,128)(2,1)}, bf16[512,4096]{1,0:T(8,128)(2,1)S(1)}) conditional(s32[]{:T(128)} %convert_element_type.174, (bf16[512,1024]{1,0:T(8,128)(2,1)}, bf16[4096,1024]{1,0:T(8,128)(2,1)}) %tuple.145, (bf16[512,4096]{1,0:T(8,128)(2,1)}, bf16[4096,1024]{1,0:T(8,128)(2,1)}) %tuple.146), branch_computations={%region_5.0_spmd, %region_6.0_spmd} | conditional | flops 4297064448 | bytes 17825810 | solution.py:80
  191.9 10.1 %convolution_convert_fusion.5 = bf16[512,1024]{1,0:T(8,128)(2,1)} fusion(bf16[512,4096]{1,0:T(8,128)(2,1)} %get-tuple-element.113, bf16[4096,1024]{1,0:T(8,128)(2,1)} %get-tuple-element.114), kind=kOutput, calls=%fused_computation.5 | convolution fusion | flops 4295491584 | bytes 13631488 | tf_op jit(solution)/shard_map/phase_a/cond/branch_1_fun/dot_general | solution.py:71
  210.4 13.5 %conditional.16 = (bf16[512,1024]{1,0:T(8,128)(2,1)S(1)}, f32[512,4096]{1,0:T(8,128)}) conditional(s32[]{:T(128)} %convert_element_type.174, (bf16[512,1024]{1,0:T(8,128)(2,1)S(1)}, bf16[4096,1024]{1,0:T(8,128)(2,1)}) %tuple.147, (bf16[512,4096]{1,0:T(8,128)(2,1)}, bf16[4096,1024]{1,0:T(8,128)(2,1)}) %tuple.148), branch_computations={%region_7.0_spmd, %region_8.0_spmd} | conditional | flops 4299161600 | bytes 22020116 | solution.py:80
  210.4 9.1 %convolution_convert_fusion.7 = bf16[512,1024]{1,0:T(8,128)(2,1)S(1)} fusion(bf16[512,4096]{1,0:T(8,128)(2,1)} %get-tuple-element.117, bf16[4096,1024]{1,0:T(8,128)(2,1)} %get-tuple-element.118), kind=kOutput, calls=%fused_computation.8 | convolution fusion | flops 4295491584 | bytes 13631488 | tf_op jit(solution)/shard_map/phase_a/cond/branch_1_fun/dot_general | solution.py:71
  233.1 9.9 %abs_reduce_fusion.1 = (f32[8,4096]{1,0:T(8,128)S(1)}, f32[8,64,4096]{2,1,0:T(8,128)}) fusion(f32[8,4096]{1,0:T(8,128)S(1)} %broadcast_bitcast_fusion.4, s32[1,2,8,64,4096]{4,3,2,1,0:T(8,128)} %param.25, bf16[8,64,4096]{2,1,0:T(8,128)(2,1)S(1)} %copy-done.2, f32[8,4096]{1,0:T(8,128)S(1)} %broadcast_bitcast_fusion.5, ...), kind=kLoop, calls=%fused_computation.99 | loop fusion | flops 23035904 | bytes 33947648 | tf_op jit(solution)/shard_map/phase_a/reduce_max | solution.py:125
  243.1 15.9 %pmax.14 = f32[8,32]{0,1:T(8,128)S(1)} all-reduce(f32[8,32]{0,1:T(8,128)S(1)} %bitcast_reduce_fusion.1), channel_id=1, replica_groups=mesh['dp'=4,'section'=2,'tensor'=4] {'tensor'}, use_global_device_ids=true, to_apply=%region_11.0 | all-reduce | flops 256 | bytes 2048 | tf_op jit(solution)/shard_map/phase_a/pmax | solution.py:126
  259.2 9.0 %multiply_convert_fusion.1 = bf16[8,64,4096]{2,1,0:T(8,128)(2,1)S(1)} fusion(f32[8,64,4096]{2,1,0:T(8,128)} %get-tuple-element.191, f32[8,4096]{1,0:T(8,128)S(1)} %get-tuple-element.210, f32[8,4096]{1,0:T(8,128)S(1)} %get-tuple-element.211), kind=kLoop, calls=%fused_computation.89 | loop fusion | flops 56623104 | bytes 12845056 | tf_op jit(solution)/shard_map/phase_a/convert_element_type | solution.py:131
  271.6 10.5 %add_convert_fusion.1 = bf16[512,4096]{1,0:T(8,128)(2,1)} fusion(f32[512,4096]{1,0:T(8,128)} %get-tuple-element.177, bf16[512,4096]{1,0:T(8,128)(2,1)} %collective-permute-done.12, bf16[512,4096]{1,0:T(8,128)(2,1)} %collective-permute-done.11, bf16[512,4096]{1,0:T(8,128)(2,1)} %collective-permute-done.10), kind=kLoop, calls=%fused_computation.86 | loop fusion | flops 14680064 | bytes 25165824 | tf_op jit(solution)/shard_map/phase_a/convert_element_type | solution.py:135
  310.7 34.6 %collective-permute-done.13 = bf16[8,64,4096]{2,1,0:T(8,128)(2,1)S(1)} collective-permute-done((bf16[8,64,4096]{2,1,0:T(8,128)(2,1)S(1)}, bf16[8,64,4096]{2,1,0:T(8,128)(2,1)S(1)}, u32[]{:S(2)}, u32[]{:S(2)}) %collective-permute-start.13) | collective-permute-done | bytes 4194336 | tf_op jit(solution)/shard_map/phase_a/ppermute | solution.py:160
  357.1 18.8 %collective-permute-done.14 = bf16[512,1024]{1,0:T(8,128)(2,1)} collective-permute-done((bf16[512,1024]{1,0:T(8,128)(2,1)S(1)}, bf16[512,1024]{1,0:T(8,128)(2,1)}, u32[]{:S(2)}, u32[]{:S(2)}) %collective-permute-start.14) | collective-permute-done | bytes 1048608 | tf_op jit(solution)/shard_map/phase_a/ppermute | solution.py:55
  379.9 19.3 %collective-permute-done.20 = bf16[512,1024]{1,0:T(8,128)(2,1)} collective-permute-done((bf16[512,1024]{1,0:T(8,128)(2,1)S(1)}, bf16[512,1024]{1,0:T(8,128)(2,1)}, u32[]{:S(2)}, u32[]{:S(2)}) %collective-permute-start.20) | collective-permute-done | bytes 1048608 | tf_op jit(solution)/shard_map/phase_a/ppermute | solution.py:55
  399.3 24.0 %conditional.21 = (bf16[4096,1024]{1,0:T(8,128)(2,1)}) conditional(s32[]{:T(128)} %convert_element_type.174, (bf16[512,4096]{1,0:T(8,128)(2,1)}, bf16[512,4096]{1,0:T(8,128)(2,1)}, bf16[512,4096]{1,0:T(8,128)(2,1)}, bf16[512,4096]{1,0:T(8,128)(2,1)}, bf16[512,1024]{1,0:T(8,128)(2,1)S(1)}, /*index=5*/bf16[512,1024]{1,0:T(8,128)(2,1)}, ...), branch_computations={%region_26.27_spmd, %region_27.28_spmd} | conditional | flops 17263755264 | bytes 29360136
  399.5 23.8 %fusion.18 = bf16[4096,1024]{1,0:T(8,128)(2,1)} fusion(bf16[512,4096]{1,0:T(8,128)(2,1)} %get-tuple-element.146, bf16[512,4096]{1,0:T(8,128)(2,1)} %get-tuple-element.145, bf16[512,4096]{1,0:T(8,128)(2,1)} %get-tuple-element.144, bf16[512,4096]{1,0:T(8,128)(2,1)} %get-tuple-element.143, bf16[512,1024]{1,0:T(8,128)(2,1)} %get-tuple-element.150, ...), kind=kOutput, calls=%fused_computation.34 | convolution fusion | flops 17263755264 | bytes 29360128 | tf_op jit(solution)/shard_map/weight_grad/cond/branch_1_fun/dot_general | solution.py:167
  423.3 10.8 %conditional.17 = (bf16[512,1024]{1,0:T(8,128)(2,1)S(1)}, bf16[512,4096]{1,0:T(8,128)(2,1)}) conditional(s32[]{:T(128)} %convert_element_type.182, (bf16[512,1024]{1,0:T(8,128)(2,1)}, bf16[4096,1024]{1,0:T(8,128)(2,1)}) %tuple.149, (bf16[512,4096]{1,0:T(8,128)(2,1)}, bf16[4096,1024]{1,0:T(8,128)(2,1)}) %tuple.150), branch_computations={%region_14.15_spmd, %region_15.16_spmd} | conditional | flops 4297064448 | bytes 17825810 | solution.py:80
  423.7 10.2 %convolution_convert_fusion.8 = bf16[512,4096]{1,0:T(8,128)(2,1)} fusion(bf16[512,1024]{1,0:T(8,128)(2,1)} %get-tuple-element.119, bf16[4096,1024]{1,0:T(8,128)(2,1)} %get-tuple-element.120), kind=kOutput, calls=%fused_computation.9 | convolution fusion | flops 4297064448 | bytes 13631488 | tf_op jit(solution)/shard_map/phase_b/cond/branch_0_fun/dot_general | solution.py:75
  436.6 10.6 %conditional.18 = (bf16[512,1024]{1,0:T(8,128)(2,1)S(1)}, bf16[512,4096]{1,0:T(8,128)(2,1)}) conditional(s32[]{:T(128)} %convert_element_type.182, (bf16[512,1024]{1,0:T(8,128)(2,1)}, bf16[4096,1024]{1,0:T(8,128)(2,1)}) %tuple.151, (bf16[512,4096]{1,0:T(8,128)(2,1)}, bf16[4096,1024]{1,0:T(8,128)(2,1)}) %tuple.152), branch_computations={%region_16.17_spmd, %region_17.18_spmd} | conditional | flops 4297064448 | bytes 17825810 | solution.py:80
  436.6 10.3 %convolution_convert_fusion.10 = bf16[512,4096]{1,0:T(8,128)(2,1)} fusion(bf16[512,1024]{1,0:T(8,128)(2,1)} %get-tuple-element.123, bf16[4096,1024]{1,0:T(8,128)(2,1)} %get-tuple-element.124), kind=kOutput, calls=%fused_computation.11 | convolution fusion | flops 4297064448 | bytes 13631488 | tf_op jit(solution)/shard_map/phase_b/cond/branch_0_fun/dot_general | solution.py:75
  449.7 11.4 %conditional.19 = (bf16[512,1024]{1,0:T(8,128)(2,1)}, bf16[512,4096]{1,0:T(8,128)(2,1)}) conditional(s32[]{:T(128)} %convert_element_type.182, (bf16[512,1024]{1,0:T(8,128)(2,1)}, bf16[4096,1024]{1,0:T(8,128)(2,1)}) %tuple.153, (bf16[512,4096]{1,0:T(8,128)(2,1)}, bf16[4096,1024]{1,0:T(8,128)(2,1)}) %tuple.154), branch_computations={%region_18.19_spmd, %region_19.20_spmd} | conditional | flops 4297064448 | bytes 17825810 | solution.py:80
  449.7 10.3 %convolution_convert_fusion.12 = bf16[512,4096]{1,0:T(8,128)(2,1)} fusion(bf16[512,1024]{1,0:T(8,128)(2,1)} %get-tuple-element.127, bf16[4096,1024]{1,0:T(8,128)(2,1)} %get-tuple-element.128), kind=kOutput, calls=%fused_computation.13 | convolution fusion | flops 4297064448 | bytes 13631488 | tf_op jit(solution)/shard_map/phase_b/cond/branch_0_fun/dot_general | solution.py:75
  467.9 10.4 %conditional.20 = (bf16[512,1024]{1,0:T(8,128)(2,1)S(1)}, f32[512,4096]{1,0:T(8,128)}) conditional(s32[]{:T(128)} %convert_element_type.182, (bf16[512,1024]{1,0:T(8,128)(2,1)S(1)}, bf16[4096,1024]{1,0:T(8,128)(2,1)}) %tuple.155, (bf16[512,4096]{1,0:T(8,128)(2,1)}, bf16[4096,1024]{1,0:T(8,128)(2,1)}) %tuple.156), branch_computations={%region_20.21_spmd, %region_21.22_spmd} | conditional | flops 4299161600 | bytes 22020116 | solution.py:80
  468.1 10.1 %fusion.1 = f32[512,4096]{1,0:T(8,128)} fusion(bf16[512,1024]{1,0:T(8,128)(2,1)S(1)} %get-tuple-element.131, bf16[4096,1024]{1,0:T(8,128)(2,1)} %get-tuple-element.132), kind=kOutput, calls=%fused_computation.16 | convolution fusion | flops 4299161600 | bytes 17825792 | tf_op jit(solution)/shard_map/phase_b/cond/branch_0_fun/dot_general | solution.py:75
  480.6 20.4 %collective-permute-done.23 = bf16[512,4096]{1,0:T(8,128)(2,1)} collective-permute-done((bf16[512,4096]{1,0:T(8,128)(2,1)}, bf16[512,4096]{1,0:T(8,128)(2,1)}, u32[]{:S(2)}, u32[]{:S(2)}) %collective-permute-start.23) | collective-permute-done | bytes 4194336 | tf_op jit(solution)/shard_map/phase_b/ppermute | solution.py:62
  501.1 55.2 %collective-permute-done.24 = bf16[512,4096]{1,0:T(8,128)(2,1)} collective-permute-done((bf16[512,4096]{1,0:T(8,128)(2,1)}, bf16[512,4096]{1,0:T(8,128)(2,1)}, u32[]{:S(2)}, u32[]{:S(2)}) %collective-permute-start.24) | collective-permute-done | bytes 4194336 | tf_op jit(solution)/shard_map/phase_b/ppermute | solution.py:62
  556.3 8.6 %add_convert_fusion = bf16[512,4096]{1,0:T(8,128)(2,1)S(1)} fusion(f32[512,4096]{1,0:T(8,128)} %get-tuple-element.185, bf16[512,4096]{1,0:T(8,128)(2,1)} %collective-permute-done.25, bf16[512,4096]{1,0:T(8,128)(2,1)} %collective-permute-done.24, bf16[512,4096]{1,0:T(8,128)(2,1)} %collective-permute-done.23), kind=kLoop, calls=%fused_computation.74 | loop fusion | flops 14680064 | bytes 25165824 | tf_op jit(solution)/shard_map/phase_b/convert_element_type | solution.py:135
  572.1 18.0 %pmax.15 = f32[8,32]{0,1:T(8,128)S(1)} all-reduce(f32[8,32]{0,1:T(8,128)S(1)} %bitcast_reduce_fusion), channel_id=1, replica_groups=mesh['dp'=4,'section'=2,'tensor'=4] {'tensor'}, use_global_device_ids=true, to_apply=%region_24.25 | all-reduce | flops 256 | bytes 2048 | tf_op jit(solution)/shard_map/phase_b/pmax | solution.py:126
  590.4 23.9 %fusion.58 = (bf16[1,8,64,4096]{3,2,1,0:T(8,128)(2,1)}, bf16[1,8,64,4096]{3,2,1,0:T(8,128)(2,1)}) fusion(bf16[8,64,4096]{2,1,0:T(8,128)(2,1)} %copy-done.6, f32[8,64,4096]{2,1,0:T(8,128)} %copy-done, bf16[8,64,4096]{2,1,0:T(8,128)(2,1)} %copy-done.8, f32[8,64]{1,0:T(8,128)S(1)} %broadcast_multiply_fusion, f32[8,64]{1,0:T(8,128)S(1)} %copy-done.18, ...), kind=kLoop, calls=%fused_computation.106 | loop fusion | flops 144703488 | bytes 50991104 | tf_op jit(solution)/shard_map/broadcast_in_dim | solution.py:194
  614.3 25.2 %reduce-scatter.2.cloned.1.call-done = bf16[1024,1024]{1,0:T(8,128)(2,1)} async-done(((bf16[4096,1024]{1,0:T(8,128)(2,1)}), bf16[1024,1024]{1,0:T(8,128)(2,1)}) %reduce-scatter.2.cloned.1.call-update) | async-done | bytes 2097168 | tf_op jit(solution)/shard_map/weight_grad/reduce_scatter | solution.py:180
  (155 shorter events, 139.8 us)
Async XLA Ops:
  7.2 155.7 %all-gather.3.cloned.1.call-start = ((), (), s32[]{:S(2)}) async-start(), calls=%async_computation.2 | async-start | bytes 10485760 | tf_op jit(solution)/shard_map/all_gather | solution.py:67
  10.3 629.1 %reduce-scatter.2.cloned.1.call-start = ((), (), s32[]{:S(2)}) async-start(), calls=%async_computation.1 | async-start | bytes 10485760 | tf_op jit(solution)/shard_map/weight_grad/reduce_scatter | solution.py:180
  23.1 139.7 %collective-permute-start.1 = (bf16[512,4096]{1,0:T(8,128)(2,1)}, bf16[512,4096]{1,0:T(8,128)(2,1)}, u32[]{:S(2)}, u32[]{:S(2)}) collective-permute-start(bf16[512,4096]{1,0:T(8,128)(2,1)} %bitcast.5), channel_id=1, source_target_pairs={{0,8},{8,0},{16,24},{24,16},{1,9},{9,1},{17,25},{25,17},{2,10},{10... | collective-permute-start | bytes 12582920 | tf_op jit(solution)/shard_map/phase_a/ppermute | solution.py:55
  28.5 148.6 %collective-permute-start.4 = (bf16[512,4096]{1,0:T(8,128)(2,1)}, bf16[512,4096]{1,0:T(8,128)(2,1)}, u32[]{:S(2)}, u32[]{:S(2)}) collective-permute-start(bf16[512,4096]{1,0:T(8,128)(2,1)} %bitcast.5), channel_id=1, source_target_pairs={{0,16},{8,24},{16,0},{24,8},{1,17},{9,25},{17,1},{25,9},{2,18},{10... | collective-permute-start | bytes 12582920 | tf_op jit(solution)/shard_map/phase_a/ppermute | solution.py:55
  31.9 159.5 %collective-permute-start.7 = (bf16[512,4096]{1,0:T(8,128)(2,1)}, bf16[512,4096]{1,0:T(8,128)(2,1)}, u32[]{:S(2)}, u32[]{:S(2)}) collective-permute-start(bf16[512,4096]{1,0:T(8,128)(2,1)} %bitcast.5), channel_id=1, source_target_pairs={{0,24},{8,16},{16,8},{24,0},{1,25},{9,17},{17,9},{25,1},{2,26},{10... | collective-permute-start | bytes 12582920 | tf_op jit(solution)/shard_map/phase_a/ppermute | solution.py:55
  37.7 2.4 collective-permute-start
  38.4 138.6 %collective-permute-start.3 = (bf16[512,1024]{1,0:T(8,128)(2,1)}, bf16[512,1024]{1,0:T(8,128)(2,1)}, u32[]{:S(2)}, u32[]{:S(2)}) collective-permute-start(bf16[512,1024]{1,0:T(8,128)(2,1)} %get-tuple-element.202), channel_id=1, source_target_pairs={{4,20},{12,28},{20,4},{28,12},{5,21},{13,29},{21,5},{29,13},{6,22}... | collective-permute-start | bytes 3145736 | tf_op jit(solution)/shard_map/phase_a/ppermute | solution.py:55
  41.1 150.3 %collective-permute-start.6 = (bf16[512,1024]{1,0:T(8,128)(2,1)S(1)}, bf16[512,1024]{1,0:T(8,128)(2,1)}, u32[]{:S(2)}, u32[]{:S(2)}) collective-permute-start(bf16[512,1024]{1,0:T(8,128)(2,1)S(1)} %get-tuple-element.201), channel_id=1, source_target_pairs={{4,28},{12,20},{20,12},{28,4},{5,29},{13,21},{21,13},{29,5},{6,30}... | collective-permute-start | bytes 3145736 | tf_op jit(solution)/shard_map/phase_a/ppermute | solution.py:55
  173.6 50.3 %collective-permute-start.2 = (bf16[512,1024]{1,0:T(8,128)(2,1)}, bf16[512,1024]{1,0:T(8,128)(2,1)}, u32[]{:S(2)}, u32[]{:S(2)}) collective-permute-start(bf16[512,1024]{1,0:T(8,128)(2,1)} %get-tuple-element.170), channel_id=1, source_target_pairs={{0,8},{8,0},{16,24},{24,16},{1,9},{9,1},{17,25},{25,17},{2,10},{10... | collective-permute-start | bytes 3145736 | tf_op jit(solution)/shard_map/phase_a/ppermute | solution.py:62
  188.0 40.8 %collective-permute-start.5 = (bf16[512,1024]{1,0:T(8,128)(2,1)}, bf16[512,1024]{1,0:T(8,128)(2,1)}, u32[]{:S(2)}, u32[]{:S(2)}) collective-permute-start(bf16[512,1024]{1,0:T(8,128)(2,1)} %get-tuple-element.171), channel_id=1, source_target_pairs={{0,16},{8,24},{16,0},{24,8},{1,17},{9,25},{17,1},{25,9},{2,18},{10... | collective-permute-start | bytes 3145736 | tf_op jit(solution)/shard_map/phase_a/ppermute | solution.py:62
  202.5 29.1 %collective-permute-start.8 = (bf16[512,1024]{1,0:T(8,128)(2,1)}, bf16[512,1024]{1,0:T(8,128)(2,1)}, u32[]{:S(2)}, u32[]{:S(2)}) collective-permute-start(bf16[512,1024]{1,0:T(8,128)(2,1)} %get-tuple-element.172), channel_id=1, source_target_pairs={{0,24},{8,16},{16,8},{24,0},{1,25},{9,17},{17,9},{25,1},{2,26},{10... | collective-permute-start | bytes 3145736 | tf_op jit(solution)/shard_map/phase_a/ppermute | solution.py:62
  205.1 28.0 %copy-start.9 = (f32[8,4096]{1,0:T(8,128)}, f32[8,4096]{1,0:T(8,128)S(1)}, u32[]{:S(2)}) copy-start(f32[8,4096]{1,0:T(8,128)S(1)} %broadcast_bitcast_fusion.4) | copy-start | bytes 393220
  205.1 66.5 %collective-permute-start.10 = (bf16[512,4096]{1,0:T(8,128)(2,1)}, bf16[512,4096]{1,0:T(8,128)(2,1)}, u32[]{:S(2)}, u32[]{:S(2)}) collective-permute-start(bf16[512,4096]{1,0:T(8,128)(2,1)} %copy-done.19), channel_id=1, source_target_pairs={{4,12},{12,4},{20,28},{28,20},{5,13},{13,5},{21,29},{29,21},{6,14}... | collective-permute-start | bytes 12582920 | tf_op jit(solution)/shard_map/phase_a/ppermute | solution.py:62
  207.7 63.9 %collective-permute-start.11 = (bf16[512,4096]{1,0:T(8,128)(2,1)}, bf16[512,4096]{1,0:T(8,128)(2,1)}, u32[]{:S(2)}, u32[]{:S(2)}) collective-permute-start(bf16[512,4096]{1,0:T(8,128)(2,1)} %copy-done.20), channel_id=1, source_target_pairs={{4,20},{12,28},{20,4},{28,12},{5,21},{13,29},{21,5},{29,13},{6,22}... | collective-permute-start | bytes 12582920 | tf_op jit(solution)/shard_map/phase_a/ppermute | solution.py:62
  223.9 47.6 %collective-permute-start.12 = (bf16[512,4096]{1,0:T(8,128)(2,1)}, bf16[512,4096]{1,0:T(8,128)(2,1)}, u32[]{:S(2)}, u32[]{:S(2)}) collective-permute-start(bf16[512,4096]{1,0:T(8,128)(2,1)} %copy-done.21), channel_id=1, source_target_pairs={{4,28},{12,20},{20,12},{28,4},{5,29},{13,21},{21,13},{29,5},{6,30}... | collective-permute-start | bytes 12582920 | tf_op jit(solution)/shard_map/phase_a/ppermute | solution.py:62
  268.3 13.8 %collective-permute-start.9 = (bf16[8,64,4096]{2,1,0:T(8,128)(2,1)S(1)}, bf16[8,64,4096]{2,1,0:T(8,128)(2,1)}, u32[]{:S(2)}, u32[]{:S(2)}) collective-permute-start(bf16[8,64,4096]{2,1,0:T(8,128)(2,1)S(1)} %multiply_convert_fusion.1), channel_id=1, source_target_pairs={{0,4},{1,5},{2,6},{3,7},{8,12},{9,13},{10,14},{11,15},{16,20},{17,... | collective-permute-start | bytes 12582920 | tf_op jit(solution)/shard_map/phase_a/ppermute | solution.py:155
  301.4 43.9 %collective-permute-start.13 = (bf16[8,64,4096]{2,1,0:T(8,128)(2,1)S(1)}, bf16[8,64,4096]{2,1,0:T(8,128)(2,1)S(1)}, u32[]{:S(2)}, u32[]{:S(2)}) collective-permute-start(bf16[8,64,4096]{2,1,0:T(8,128)(2,1)S(1)} %fusion.37), channel_id=1, source_target_pairs={{4,0},{5,1},{6,2},{7,3},{12,8},{13,9},{14,10},{15,11},{20,16},{21,... | collective-permute-start | bytes 12582920 | tf_op jit(solution)/shard_map/phase_a/ppermute | solution.py:160
  302.7 51.1 %collective-permute-start.15 = (bf16[512,4096]{1,0:T(8,128)(2,1)}, bf16[512,4096]{1,0:T(8,128)(2,1)}, u32[]{:S(2)}, u32[]{:S(2)}) collective-permute-start(bf16[512,4096]{1,0:T(8,128)(2,1)} %bitcast.16), channel_id=1, source_target_pairs={{4,12},{12,4},{20,28},{28,20},{5,13},{13,5},{21,29},{29,21},{6,14}... | collective-permute-start | bytes 12582920 | tf_op jit(solution)/shard_map/phase_a/ppermute | solution.py:55
  305.4 51.7 %collective-permute-start.18 = (bf16[512,4096]{1,0:T(8,128)(2,1)}, bf16[512,4096]{1,0:T(8,128)(2,1)}, u32[]{:S(2)}, u32[]{:S(2)}) collective-permute-start(bf16[512,4096]{1,0:T(8,128)(2,1)} %bitcast.16), channel_id=1, source_target_pairs={{4,20},{12,28},{20,4},{28,12},{5,21},{13,29},{21,5},{29,13},{6,22}... | collective-permute-start | bytes 12582920 | tf_op jit(solution)/shard_map/phase_a/ppermute | solution.py:55
  308.0 49.1 %collective-permute-start.21 = (bf16[512,4096]{1,0:T(8,128)(2,1)}, bf16[512,4096]{1,0:T(8,128)(2,1)}, u32[]{:S(2)}, u32[]{:S(2)}) collective-permute-start(bf16[512,4096]{1,0:T(8,128)(2,1)} %bitcast.16), channel_id=1, source_target_pairs={{4,28},{12,20},{20,12},{28,4},{5,29},{13,21},{21,13},{29,5},{6,30}... | collective-permute-start | bytes 12582920 | tf_op jit(solution)/shard_map/phase_a/ppermute | solution.py:55
  347.8 28.0 %collective-permute-start.14 = (bf16[512,1024]{1,0:T(8,128)(2,1)S(1)}, bf16[512,1024]{1,0:T(8,128)(2,1)}, u32[]{:S(2)}, u32[]{:S(2)}) collective-permute-start(bf16[512,1024]{1,0:T(8,128)(2,1)S(1)} %get-tuple-element.196), channel_id=1, source_target_pairs={{0,8},{8,0},{16,24},{24,16},{1,9},{9,1},{17,25},{25,17},{2,10},{10... | collective-permute-start | bytes 3145736 | tf_op jit(solution)/shard_map/phase_a/ppermute | solution.py:55
  350.3 29.6 %collective-permute-start.17 = (bf16[512,1024]{1,0:T(8,128)(2,1)S(1)}, bf16[512,1024]{1,0:T(8,128)(2,1)}, u32[]{:S(2)}, u32[]{:S(2)}) collective-permute-start(bf16[512,1024]{1,0:T(8,128)(2,1)S(1)} %get-tuple-element.199), channel_id=1, source_target_pairs={{0,16},{8,24},{16,0},{24,8},{1,17},{9,25},{17,1},{25,9},{2,18},{10... | collective-permute-start | bytes 3145736 | tf_op jit(solution)/shard_map/phase_a/ppermute | solution.py:55
  353.7 45.5 %collective-permute-start.20 = (bf16[512,1024]{1,0:T(8,128)(2,1)S(1)}, bf16[512,1024]{1,0:T(8,128)(2,1)}, u32[]{:S(2)}, u32[]{:S(2)}) collective-permute-start(bf16[512,1024]{1,0:T(8,128)(2,1)S(1)} %get-tuple-element.198), channel_id=1, source_target_pairs={{0,24},{8,16},{16,8},{24,0},{1,25},{9,17},{17,9},{25,1},{2,26},{10... | collective-permute-start | bytes 3145736 | tf_op jit(solution)/shard_map/phase_a/ppermute | solution.py:55
  434.1 67.0 %collective-permute-start.23 = (bf16[512,4096]{1,0:T(8,128)(2,1)}, bf16[512,4096]{1,0:T(8,128)(2,1)}, u32[]{:S(2)}, u32[]{:S(2)}) collective-permute-start(bf16[512,4096]{1,0:T(8,128)(2,1)} %get-tuple-element.182), channel_id=1, source_target_pairs={{0,8},{8,0},{16,24},{24,16},{1,9},{9,1},{17,25},{25,17},{2,10},{10... | collective-permute-start | bytes 12582920 | tf_op jit(solution)/shard_map/phase_b/ppermute | solution.py:62
  447.2 109.1 %collective-permute-start.24 = (bf16[512,4096]{1,0:T(8,128)(2,1)}, bf16[512,4096]{1,0:T(8,128)(2,1)}, u32[]{:S(2)}, u32[]{:S(2)}) collective-permute-start(bf16[512,4096]{1,0:T(8,128)(2,1)} %get-tuple-element.183), channel_id=1, source_target_pairs={{0,16},{8,24},{16,0},{24,8},{1,17},{9,25},{17,1},{25,9},{2,18},{10... | collective-permute-start | bytes 12582920 | tf_op jit(solution)/shard_map/phase_b/ppermute | solution.py:62
  461.1 95.2 %collective-permute-start.25 = (bf16[512,4096]{1,0:T(8,128)(2,1)}, bf16[512,4096]{1,0:T(8,128)(2,1)}, u32[]{:S(2)}, u32[]{:S(2)}) collective-permute-start(bf16[512,4096]{1,0:T(8,128)(2,1)} %get-tuple-element.184), channel_id=1, source_target_pairs={{0,24},{8,16},{16,8},{24,0},{1,25},{9,17},{17,9},{25,1},{2,26},{10... | collective-permute-start | bytes 12582920 | tf_op jit(solution)/shard_map/phase_b/ppermute | solution.py:62
  465.4 1.5 collective-permute-start.16
  466.1 14.0 %collective-permute-start.19 = (bf16[512,1024]{1,0:T(8,128)(2,1)}, bf16[512,1024]{1,0:T(8,128)(2,1)S(1)}, u32[]{:S(2)}, u32[]{:S(2)}) collective-permute-start(bf16[512,1024]{1,0:T(8,128)(2,1)} %copy-done.16), channel_id=1, source_target_pairs={{4,20},{12,28},{20,4},{28,12},{5,21},{13,29},{21,5},{29,13},{6,22}... | collective-permute-start | bytes 3145736 | tf_op jit(solution)/shard_map/phase_b/ppermute | solution.py:62
  466.9 13.4 %collective-permute-start.22 = (bf16[512,1024]{1,0:T(8,128)(2,1)}, bf16[512,1024]{1,0:T(8,128)(2,1)S(1)}, u32[]{:S(2)}, u32[]{:S(2)}) collective-permute-start(bf16[512,1024]{1,0:T(8,128)(2,1)} %get-tuple-element.180), channel_id=1, source_target_pairs={{4,28},{12,20},{20,12},{28,4},{5,29},{13,21},{21,13},{29,5},{6,30}... | collective-permute-start | bytes 3145736 | tf_op jit(solution)/shard_map/phase_b/ppermute | solution.py:62
  480.3 84.7 %slice-start = ((s8[8388608]{0:T(1024)(128)(4,1)}), s8[4194304]{0:T(1024)(128)(4,1)S(1)}, s32[]{:S(2)}) async-start(s8[8388608]{0:T(1024)(128)(4,1)} %bitcast.100), calls=%async_computation.3 | async-start | bytes 8388608
  480.6 84.4 %copy-start.3 = (bf16[512,4096]{1,0:T(8,128)(2,1)}, bf16[512,4096]{1,0:T(8,128)(2,1)S(1)}, u32[]{:S(2)}) copy-start(bf16[512,4096]{1,0:T(8,128)(2,1)S(1)} %constant_dynamic-update-slice_fusion) | copy-start | bytes 12582916
  565.0 25.3 %copy-start.12 = (f32[8,4096]{1,0:T(8,128)S(1)}, f32[8,4096]{1,0:T(8,128)}, u32[]{:S(2)}) copy-start(f32[8,4096]{1,0:T(8,128)} %copy-done.11) | copy-start | bytes 393220
  (25 other events, 241.4 us)
Sparse Core Ops, SparseCore 0:
  10.4 152.3 all-gather.2
  423.4 216.0 reduce-scatter.1

commit v2 on v1

--- a/solution.py
+++ b/solution.py
@@ -79,10 +79,19 @@
 
         return lax.cond(forward_here, forward, backward, whole, piece)
 
+    relayed = dp_count == 4
+    half = tokens // 2
+
     def pre(normed, upstream, forward_section):
         whole, piece = [normed], [columns(upstream, replica)]
         for step in range(1, dp_count):
-            whole.append(exchange(normed, forward_section, step))
+            if relayed and step == 3:
+                whole.append(jnp.concatenate([
+                    exchange(whole[1][:half], forward_section, 2),
+                    exchange(whole[2][half:], forward_section, 1),
+                ], axis=0))
+            else:
+                whole.append(exchange(normed, forward_section, step))
             piece.append(
                 exchange(columns(upstream, target(replica, step)), 1 - forward_section, step)
             )
@@ -91,18 +100,49 @@
     def middle(whole, piece, forward_section):
         here = first if forward_section == 0 else ~first
         branch = jnp.zeros((tokens, width), bf16)
-        grad = None
-        order = list(range(1, dp_count)) + [0]
-        for step in order:
-            out, back = product(here, whole[step], piece[step])
-            if step:
-                out = give_back(out, forward_section, step)
-                back = give_back(back, 1 - forward_section, step)
+        steps = list(range(1, dp_count)) + [0]
+        forward_order = steps if forward_section == 0 else sorted(steps)
+        backward_order = [3, 1, 2, 0] if relayed else steps
+        top, bottom = [], []
+
+        def home(value, step):
+            return give_back(value, 1 - forward_section, step)
+
+        def plus(value, other):
+            return (value.astype(f32) + other.astype(f32)).astype(bf16)
+
+        for ahead, behind in zip(forward_order, backward_order):
+            out, back = product(here, whole[ahead], piece[behind])
+            if ahead:
+                out = give_back(out, forward_section, ahead)
             branch = lax.dynamic_update_slice_in_dim(
-                branch, out, target(replica, step) * part, 1
-            )
-            grad = back.astype(f32) if grad is None else grad + back.astype(f32)
+                branch, out, target(replica, ahead) * part, 1
+            )
+            upper, lower = back[:half], back[half:]
+            if relayed and behind == 3:
+                relay_upper, relay_lower = home(upper, 1), home(lower, 2)
+                continue
+            if relayed and behind == 1:
+                lower = plus(lower, relay_lower)
+            if relayed and behind == 2:
+                upper = plus(upper, relay_upper)
+            if behind:
+                upper, lower = home(upper, behind), home(lower, behind)
+            top.append(upper.astype(f32))
+            bottom.append(lower.astype(f32))
+        grad = jnp.concatenate([sum(top[1:], top[0]), sum(bottom[1:], bottom[0])], axis=0)
         return branch, grad
+
+    def largest(value):
+        count = lax.axis_size("tensor")
+        if count & (count - 1):
+            return lax.pmax(value, "tensor")
+        step = 1
+        while step < count:
+            pairs = [(source, source ^ step) for source in range(count)]
+            value = jnp.maximum(value, lax.ppermute(value, "tensor", pairs))
+            step *= 2
+        return value
 
     def scales_row(slot, chunk):
         now = cache_scales[0, slot, chunk * micros:(chunk + 1) * micros, 0]
@@ -123,7 +163,7 @@
     def finish_forward(hidden, branch, chunk):
         delta = hidden + shaped(branch).astype(f32) - codes(1, chunk) * scales_row(1, chunk)
         peak = jnp.max(jnp.abs(delta), axis=1).reshape(micros, block_count, block).max(axis=-1)
-        spread = lax.pmax(peak, "tensor") + epsilon
+        spread = largest(peak) + epsilon
         up_scale = jnp.repeat(code_levels / spread, block, axis=-1)[:, None, :]
         down_scale = jnp.repeat(spread / code_levels, block, axis=-1)[:, None, :]
         level = delta * up_scale
@@ -161,25 +201,29 @@
             stage_b.append((hidden, upstream, pre(normed, flat(upstream), 1)))
 
     with jax.named_scope("weight_grad"):
-        def gathered(pairs):
+        def gathered(pairs, start):
             whole = jnp.concatenate([w for p in pairs for w in p[0]], axis=0)
-            piece = jnp.concatenate([g for p in pairs for g in p[1]], axis=0)
+            piece = jnp.concatenate(
+                [g[:, start:start + slab] for p in pairs for g in p[1]], axis=0
+            )
             return lax.dot_general(
                 whole, piece, (((0,), (0,)), ((), ())), preferred_element_type=f32
             ).astype(bf16)
 
+        slab = part // 2
         from_a = [a[1] for a in stage_a]
         from_b = [b[2] for b in stage_b]
-        partial = lax.cond(
-            first,
-            lambda a, b: gathered([(x[0], y[1]) for x, y in zip(a, b)]),
-            lambda a, b: gathered([(y[0], x[1]) for x, y in zip(a, b)]),
-            from_a,
-            from_b,
-        )
-        weight_grad = lax.psum_scatter(
-            partial, "tensor", scatter_dimension=0, tiled=True
-        ).astype(f32)
+        summed = []
+        for start in (0, slab):
+            partial = lax.cond(
+                first,
+                lambda a, b: gathered([(x[0], y[1]) for x, y in zip(a, b)], start),
+                lambda a, b: gathered([(y[0], x[1]) for x, y in zip(a, b)], start),
+                from_a,
+                from_b,
+            )
+            summed.append(lax.psum_scatter(partial, "tensor", scatter_dimension=0, tiled=True))
+        weight_grad = jnp.concatenate(summed, axis=1).astype(f32)
 
     with jax.named_scope("phase_b"):
         for c in over:

time: 660 us -> 638 us (0.967)
  waiting for transfers between devices: 299 us -> 257 us
  local copies, waits for them, and re-layouts: 29.3 us -> 66.7 us
  blocking collectives: 33.9 us -> 0 us
  starting transfers between devices: 65.6 us -> 87.2 us
    all_gather x1, waiting for transfers between devices: 120 us -> 33.4 us  [local(): lax.all_gather(columns(weight[0], replica), 'tensor', axis=0, tiled=True)]
    ppermute x12 -> x14, waiting for transfers between devices: 42.2 us -> 115 us  [exchange(): return lax.ppermute(value, ('dp', 'section'), pairs)]
    ppermute x12 -> x18, waiting for transfers between devices: 77.2 us -> 5.78 us  [give_back(): return lax.ppermute(value, ('dp', 'section'), pairs)]
    pmax x2 -> x0, blocking collectives: 33.9 us -> none  [finish_forward(): spread = lax.pmax(peak, 'tensor') + epsilon]
    reduce_scatter x1 -> x2, waiting for transfers between devices: 25.2 us -> 48.6 us  [local(): lax.psum_scatter(partial, 'tensor', scatter_dimension=0, tiled=True)]
    slice x0 -> x18, local copies, waits for them, and re-layouts: none -> 20.6 us  [the longest x6 7.85 us: middle(): upper, lower = (back[:half], back[half:])]
    ppermute x12 -> x18, starting transfers between devices: 28.9 us -> 40.8 us  [give_back(): return lax.ppermute(value, ('dp', 'section'), pairs)]
    ppermute x1, waiting for transfers between devices: 34.6 us -> 45.4 us  [local(): upstream = lax.ppermute(grads[c], 'section', [(1, 0)])]
  transfers between devices with their start and end apart: 28 -> 41, of which waited for: 9 -> 13; matrix products, arithmetic and copies ran while one was open for 28% -> 34% of each run, Pallas kernels for 0% -> 0%
where the time goes in v2:
time: 638 us; the launch traced here: 631 us
  waiting for transfers between devices  257 us (40%)
  other arithmetic  103 us (16%)
  matrix products  99.1 us (16%)
  starting transfers between devices  87.2 us (14%)
  local copies, waits for them, and re-layouts  66.7 us (10%)
  between operations  15.3 us (2%)
    ppermute x14, waiting for transfers between devices, exchange(): return lax.ppermute(value, ('dp', 'section'), pairs)  115 us
    reduce_scatter x2, waiting for transfers between devices, local(): lax.psum_scatter(partial, 'tensor', scatter_dimension=0, tiled=True)  48.6 us
    ppermute x1, waiting for transfers between devices, local(): upstream = lax.ppermute(grads[c], 'section', [(1, 0)])  45.4 us
    ppermute x18, starting transfers between devices, give_back(): return lax.ppermute(value, ('dp', 'section'), pairs)  40.8 us
    dot_general x4, matrix products, forward(): out = jnp.dot(whole, weight_part, preferred_element_type=f32).astype(bf16)  38.8 us
    ppermute x14, starting transfers between devices, exchange(): return lax.ppermute(value, ('dp', 'section'), pairs)  37.3 us
    all_gather x1, waiting for transfers between devices, local(): lax.all_gather(columns(weight[0], replica), 'tensor', axis=0, tiled=True)  33.4 us
    dot_general x4, matrix products, backward(): lax.dot_general(piece, weight_part, (((1,), (1,)), ((), ())), preferred_e...  32.9 us
  transfers between devices with their start and end apart: 41, of which 13 were waited for; matrix products, arithmetic and copies ran while one was open for 34% of the time, Pallas kernels for 0%

profile of v2, /device:TPU:0, one launch (start us, length us, event | category | flops | bytes accessed | tf_op | source)
XLA Modules:
  0.0 630.6 jit_solution(15036750423383025089)
XLA Ops:
  31.0 65.5 %collective-permute-done.1 = bf16[512,4096]{1,0:T(8,128)(2,1)S(1)} collective-permute-done((bf16[512,4096]{1,0:T(8,128)(2,1)S(1)}, bf16[512,4096]{1,0:T(8,128)(2,1)S(1)}, u32[]{:S(2)}, u32[]{:S(2)}) %collective-permute-start.1) | collective-permute-done | bytes 4194336 | tf_op jit(solution)/shard_map/phase_a/ppermute | solution.py:55
  117.9 8.4 %collective-permute-done.7 = bf16[256,4096]{1,0:T(8,128)(2,1)} collective-permute-done((bf16[256,4096]{1,0:T(8,128)(2,1)}, bf16[256,4096]{1,0:T(8,128)(2,1)}, u32[]{:S(2)}, u32[]{:S(2)}) %collective-permute-start.7) | collective-permute-done | bytes 2097184 | tf_op jit(solution)/shard_map/phase_a/ppermute | solution.py:55
  129.4 33.4 %all-gather.3.cloned.1.call-done = bf16[1,4096,1024]{2,1,0:T(8,128)(2,1)} async-done(((bf16[1,1024,1024]{2,1,0:T(8,128)(2,1)}), bf16[1,4096,1024]{2,1,0:T(8,128)(2,1)}) %all-gather.3.cloned.1.call-update) | async-done | bytes 8388624 | tf_op jit(solution)/shard_map/all_gather | solution.py:67
  162.8 10.8 %conditional.18 = (bf16[512,1024]{1,0:T(8,128)(2,1)}, bf16[512,4096]{1,0:T(8,128)(2,1)S(1)}) conditional(s32[]{:T(128)} %convert_element_type.231, (bf16[512,1024]{1,0:T(8,128)(2,1)}, bf16[4096,1024]{1,0:T(8,128)(2,1)}) %tuple.173, (bf16[512,4096]{1,0:T(8,128)(2,1)}, bf16[4096,1024]{1,0:T(8,128)(2,1)}) %tuple.174), branch_computations={%region_1.0_spmd, %region_2.0_spmd} | conditional | flops 4297064448 | bytes 17825810 | solution.py:80
  163.0 10.2 %convolution_convert_fusion.1 = bf16[512,1024]{1,0:T(8,128)(2,1)} fusion(bf16[512,4096]{1,0:T(8,128)(2,1)} %get-tuple-element.140, bf16[4096,1024]{1,0:T(8,128)(2,1)} %get-tuple-element.141), kind=kOutput, calls=%fused_computation.1 | convolution fusion | flops 4295491584 | bytes 13631488 | tf_op jit(solution)/shard_map/phase_a/cond/branch_1_fun/dot_general | solution.py:71
  177.1 10.7 %conditional.19 = (bf16[512,1024]{1,0:T(8,128)(2,1)}, bf16[512,4096]{1,0:T(8,128)(2,1)S(1)}) conditional(s32[]{:T(128)} %convert_element_type.231, (bf16[512,1024]{1,0:T(8,128)(2,1)}, bf16[4096,1024]{1,0:T(8,128)(2,1)}) %tuple.175, (bf16[512,4096]{1,0:T(8,128)(2,1)}, bf16[4096,1024]{1,0:T(8,128)(2,1)}) %tuple.176), branch_computations={%region_3.0_spmd, %region_4.0_spmd} | conditional | flops 4297064448 | bytes 17825810 | solution.py:80
  177.1 10.2 %convolution_convert_fusion.3 = bf16[512,1024]{1,0:T(8,128)(2,1)} fusion(bf16[512,4096]{1,0:T(8,128)(2,1)} %get-tuple-element.144, bf16[4096,1024]{1,0:T(8,128)(2,1)} %get-tuple-element.145), kind=kOutput, calls=%fused_computation.3 | convolution fusion | flops 4295491584 | bytes 13631488 | tf_op jit(solution)/shard_map/phase_a/cond/branch_1_fun/dot_general | solution.py:71
  192.6 9.9 %conditional.20 = (bf16[512,1024]{1,0:T(8,128)(2,1)S(1)}, bf16[512,4096]{1,0:T(8,128)(2,1)S(1)}) conditional(s32[]{:T(128)} %convert_element_type.231, (bf16[512,1024]{1,0:T(8,128)(2,1)}, bf16[4096,1024]{1,0:T(8,128)(2,1)}) %tuple.177, (bf16[512,4096]{1,0:T(8,128)(2,1)}, bf16[4096,1024]{1,0:T(8,128)(2,1)}) %tuple.178), branch_computations={%region_5.0_spmd, %region_6.0_spmd} | conditional | flops 4297064448 | bytes 17825810 | solution.py:80
  192.8 9.1 %convolution_convert_fusion.5 = bf16[512,1024]{1,0:T(8,128)(2,1)S(1)} fusion(bf16[512,4096]{1,0:T(8,128)(2,1)} %get-tuple-element.148, bf16[4096,1024]{1,0:T(8,128)(2,1)} %get-tuple-element.149), kind=kOutput, calls=%fused_computation.5 | convolution fusion | flops 4295491584 | bytes 13631488 | tf_op jit(solution)/shard_map/phase_a/cond/branch_1_fun/dot_general | solution.py:71
  205.0 10.2 %conditional.21 = (bf16[512,1024]{1,0:T(8,128)(2,1)S(1)}, bf16[512,4096]{1,0:T(8,128)(2,1)S(1)}) conditional(s32[]{:T(128)} %convert_element_type.231, (bf16[512,1024]{1,0:T(8,128)(2,1)S(1)}, bf16[4096,1024]{1,0:T(8,128)(2,1)}) %tuple.179, (bf16[512,4096]{1,0:T(8,128)(2,1)}, bf16[4096,1024]{1,0:T(8,128)(2,1)}) %tuple.180), branch_computations={%region_7.0_spmd, %region_8.0_spmd} | conditional | flops 4297064448 | bytes 17825810 | solution.py:80
  205.4 9.3 %convolution_convert_fusion.7 = bf16[512,1024]{1,0:T(8,128)(2,1)S(1)} fusion(bf16[512,4096]{1,0:T(8,128)(2,1)} %get-tuple-element.152, bf16[4096,1024]{1,0:T(8,128)(2,1)} %get-tuple-element.153), kind=kOutput, calls=%fused_computation.7 | convolution fusion | flops 4295491584 | bytes 13631488 | tf_op jit(solution)/shard_map/phase_a/cond/branch_1_fun/dot_general | solution.py:71
  220.4 8.6 %abs_reduce_fusion.1 = (f32[8,4096]{1,0:T(8,128)}, f32[8,64,4096]{2,1,0:T(8,128)S(1)}) fusion(f32[8,4096]{1,0:T(8,128)} %get-tuple-element.269, s32[1,2,8,64,4096]{4,3,2,1,0:T(8,128)} %param.27, bf16[8,64,4096]{2,1,0:T(8,128)(2,1)S(1)} %copy-done.3, f32[8,4096]{1,0:T(8,128)} %copy-done.30, bf16[512,4096]{1,0:T(8,128)(2,1)S(1)} %constant_dynamic-update-slice_fusion.8), kind=kLoop, calls=%fused_computation.127 | loop fusion | flops 23035904 | bytes 33947648 | tf_op jit(solution)/shard_map/phase_a/reduce_max | solution.py:165
  241.6 7.3 %multiply_convert_fusion.1 = bf16[8,64,4096]{2,1,0:T(8,128)(2,1)S(1)} fusion(f32[8,64,4096]{2,1,0:T(8,128)S(1)} %get-tuple-element.242, f32[8,4096]{1,0:T(8,128)S(1)} %broadcast_bitcast_fusion.2, f32[8,4096]{1,0:T(8,128)S(1)} %broadcast_bitcast_fusion.3), kind=kLoop, calls=%fused_computation.117 | loop fusion | flops 56623104 | bytes 12845056 | tf_op jit(solution)/shard_map/phase_a/convert_element_type | solution.py:171
  269.8 6.0 multiply_convert_fusion.3
  293.0 45.4 %collective-permute-done.19 = bf16[8,64,4096]{2,1,0:T(8,128)(2,1)S(1)} collective-permute-done((bf16[8,64,4096]{2,1,0:T(8,128)(2,1)S(1)}, bf16[8,64,4096]{2,1,0:T(8,128)(2,1)S(1)}, u32[]{:S(2)}, u32[]{:S(2)}) %collective-permute-start.19) | collective-permute-done | bytes 4194336 | tf_op jit(solution)/shard_map/phase_a/ppermute | solution.py:200
  349.7 19.6 %collective-permute-done.20 = bf16[512,1024]{1,0:T(8,128)(2,1)S(1)} collective-permute-done((bf16[512,1024]{1,0:T(8,128)(2,1)S(1)}, bf16[512,1024]{1,0:T(8,128)(2,1)S(1)}, u32[]{:S(2)}, u32[]{:S(2)}) %collective-permute-start.20) | collective-permute-done | bytes 1048608 | tf_op jit(solution)/shard_map/phase_a/ppermute | solution.py:55
  369.3 21.5 %collective-permute-done.21 = bf16[512,1024]{1,0:T(8,128)(2,1)S(1)} collective-permute-done((bf16[512,1024]{1,0:T(8,128)(2,1)S(1)}, bf16[512,1024]{1,0:T(8,128)(2,1)S(1)}, u32[]{:S(2)}, u32[]{:S(2)}) %collective-permute-start.21) | collective-permute-done | bytes 1048608 | tf_op jit(solution)/shard_map/phase_a/ppermute | solution.py:55
  393.9 16.8 %conditional.26 = (bf16[4096,512]{1,0:T(8,128)(2,1)}) conditional(s32[]{:T(128)} %convert_element_type.231, (bf16[512,4096]{1,0:T(8,128)(2,1)S(1)}, bf16[512,4096]{1,0:T(8,128)(2,1)}, bf16[512,4096]{1,0:T(8,128)(2,1)}, bf16[512,4096]{1,0:T(8,128)(2,1)}, bf16[512,1024]{1,0:T(8,128)(2,1)S(1)}, /*index=5*/bf16[512,1024]{1,0:T(8,128)(2,1)}, ...), branch_computations={%region_24.25_spmd, %region_25.26_spmd} | conditional | flops 8665432064 | bytes 44040228
  396.7 14.0 %fusion.16 = bf16[4096,512]{1,0:T(8,128)(2,1)} fusion(bf16[512,4096]{1,0:T(8,128)(2,1)} %get-tuple-element.181, bf16[512,4096]{1,0:T(8,128)(2,1)} %get-tuple-element.180, bf16[512,4096]{1,0:T(8,128)(2,1)} %get-tuple-element.179, bf16[512,4096]{1,0:T(8,128)(2,1)S(1)} %copy-done.12, bf16[512,512]{1,0:T(8,128)(2,1)} %slice.91, bf16[512,512]{1,0:T(8,128)(2,1)} %slice.90, ...), kind=kOutput, calls=%fused_computation.32 | convolution fusion | flops 8665432064 | bytes 23068672 | tf_op jit(solution)/shard_map/weight_grad/cond/branch_1_fun/dot_general | solution.py:209
  410.8 8.3 %conditional.22 = (bf16[512,1024]{1,0:T(8,128)(2,1)S(1)}, bf16[512,4096]{1,0:T(8,128)(2,1)S(1)}) conditional(s32[]{:T(128)} %convert_element_type.239, (bf16[512,1024]{1,0:T(8,128)(2,1)S(1)}, bf16[4096,1024]{1,0:T(8,128)(2,1)}) %tuple.181, (bf16[512,4096]{1,0:T(8,128)(2,1)}, bf16[4096,1024]{1,0:T(8,128)(2,1)}) %tuple.182), branch_computations={%region_13.14_spmd, %region_14.15_spmd} | conditional | flops 4297064448 | bytes 17825810 | solution.py:80
  410.8 8.2 %convolution_convert_fusion.8 = bf16[512,4096]{1,0:T(8,128)(2,1)S(1)} fusion(bf16[512,1024]{1,0:T(8,128)(2,1)S(1)} %get-tuple-element.154, bf16[4096,1024]{1,0:T(8,128)(2,1)} %get-tuple-element.155), kind=kOutput, calls=%fused_computation.8 | convolution fusion | flops 4297064448 | bytes 13631488 | tf_op jit(solution)/shard_map/phase_b/cond/branch_0_fun/dot_general | solution.py:75
  428.0 9.9 %conditional.23 = (bf16[512,1024]{1,0:T(8,128)(2,1)}, bf16[512,4096]{1,0:T(8,128)(2,1)S(1)}) conditional(s32[]{:T(128)} %convert_element_type.239, (bf16[512,1024]{1,0:T(8,128)(2,1)S(1)}, bf16[4096,1024]{1,0:T(8,128)(2,1)}) %tuple.183, (bf16[512,4096]{1,0:T(8,128)(2,1)}, bf16[4096,1024]{1,0:T(8,128)(2,1)}) %tuple.184), branch_computations={%region_15.16_spmd, %region_16.17_spmd} | conditional | flops 4297064448 | bytes 17825810 | solution.py:80
  428.4 8.3 %convolution_convert_fusion.10 = bf16[512,4096]{1,0:T(8,128)(2,1)S(1)} fusion(bf16[512,1024]{1,0:T(8,128)(2,1)S(1)} %get-tuple-element.158, bf16[4096,1024]{1,0:T(8,128)(2,1)} %get-tuple-element.159), kind=kOutput, calls=%fused_computation.10 | convolution fusion | flops 4297064448 | bytes 13631488 | tf_op jit(solution)/shard_map/phase_b/cond/branch_0_fun/dot_general | solution.py:75
  440.1 9.5 %conditional.24 = (bf16[512,1024]{1,0:T(8,128)(2,1)}, bf16[512,4096]{1,0:T(8,128)(2,1)S(1)}) conditional(s32[]{:T(128)} %convert_element_type.239, (bf16[512,1024]{1,0:T(8,128)(2,1)}, bf16[4096,1024]{1,0:T(8,128)(2,1)}) %tuple.185, (bf16[512,4096]{1,0:T(8,128)(2,1)}, bf16[4096,1024]{1,0:T(8,128)(2,1)}) %tuple.186), branch_computations={%region_17.18_spmd, %region_18.19_spmd} | conditional | flops 4297064448 | bytes 17825810 | solution.py:80
  440.1 8.3 %convolution_convert_fusion.12 = bf16[512,4096]{1,0:T(8,128)(2,1)S(1)} fusion(bf16[512,1024]{1,0:T(8,128)(2,1)} %get-tuple-element.162, bf16[4096,1024]{1,0:T(8,128)(2,1)} %get-tuple-element.163), kind=kOutput, calls=%fused_computation.12 | convolution fusion | flops 4297064448 | bytes 13631488 | tf_op jit(solution)/shard_map/phase_b/cond/branch_0_fun/dot_general | solution.py:75
  475.2 9.3 %conditional.25 = (bf16[512,1024]{1,0:T(8,128)(2,1)}, bf16[512,4096]{1,0:T(8,128)(2,1)S(1)}) conditional(s32[]{:T(128)} %convert_element_type.239, (bf16[512,1024]{1,0:T(8,128)(2,1)S(1)}, bf16[4096,1024]{1,0:T(8,128)(2,1)}) %tuple.187, (bf16[512,4096]{1,0:T(8,128)(2,1)}, bf16[4096,1024]{1,0:T(8,128)(2,1)}) %tuple.188), branch_computations={%region_19.20_spmd, %region_20.21_spmd} | conditional | flops 4297064448 | bytes 17825810 | solution.py:80
  475.2 8.2 %convolution_convert_fusion.14 = bf16[512,4096]{1,0:T(8,128)(2,1)S(1)} fusion(bf16[512,1024]{1,0:T(8,128)(2,1)S(1)} %get-tuple-element.166, bf16[4096,1024]{1,0:T(8,128)(2,1)} %get-tuple-element.167), kind=kOutput, calls=%fused_computation.14 | convolution fusion | flops 4297064448 | bytes 13631488 | tf_op jit(solution)/shard_map/phase_b/cond/branch_0_fun/dot_general | solution.py:75
  490.9 17.5 %conditional.27 = (bf16[4096,512]{1,0:T(8,128)(2,1)}) conditional(s32[]{:T(128)} %convert_element_type.231, (bf16[512,4096]{1,0:T(8,128)(2,1)S(1)}, bf16[512,4096]{1,0:T(8,128)(2,1)}, bf16[512,4096]{1,0:T(8,128)(2,1)}, bf16[512,4096]{1,0:T(8,128)(2,1)}, bf16[512,1024]{1,0:T(8,128)(2,1)S(1)}, /*index=5*/bf16[512,1024]{1,0:T(8,128)(2,1)}, ...), branch_computations={%region_27.28_spmd, %region_28.29_spmd} | conditional | flops 8665432064 | bytes 44040228
  494.7 13.4 %fusion.48 = bf16[4096,512]{1,0:T(8,128)(2,1)} fusion(bf16[512,4096]{1,0:T(8,128)(2,1)} %get-tuple-element.197, bf16[512,4096]{1,0:T(8,128)(2,1)} %get-tuple-element.196, bf16[512,4096]{1,0:T(8,128)(2,1)} %get-tuple-element.195, bf16[512,4096]{1,0:T(8,128)(2,1)S(1)} %copy-done.13, bf16[512,512]{1,0:T(8,128)(2,1)S(1)} %slice.99, ...), kind=kOutput, calls=%fused_computation.64 | convolution fusion | flops 8665432064 | bytes 23068672 | tf_op jit(solution)/shard_map/weight_grad/cond/branch_1_fun/dot_general | solution.py:209
  530.8 7.6 %fusion.68 = (f32[8,64]{1,0:T(8,128)S(1)}, f32[8,4096]{1,0:T(8,128)S(1)}) fusion(bf16[8,64,4096]{2,1,0:T(8,128)(2,1)} %bitcast.108, f32[8,64,4096]{2,1,0:T(8,128)S(1)} %bitcast.100, f32[8,64]{1,0:T(8,128)S(1)} %copy-done.43, f32[8,4096]{1,0:T(8,128)S(1)} %copy-done.31, s32[1,2,8,64,4096]{4,3,2,1,0:T(8,128)} %param.27, ...), kind=kLoop, calls=%fused_computation.92 | loop fusion | flops 23035392 | bytes 25432064 | tf_op jit(solution)/shard_map/phase_b/reduce_sum | solution.py:177
  547.2 23.7 %fusion.88 = (bf16[1,8,64,4096]{3,2,1,0:T(8,128)(2,1)}, bf16[1,8,64,4096]{3,2,1,0:T(8,128)(2,1)}) fusion(bf16[8,64,4096]{2,1,0:T(8,128)(2,1)} %copy-done.8, f32[8,64,4096]{2,1,0:T(8,128)S(1)} %bitcast.100, bf16[8,64,4096]{2,1,0:T(8,128)(2,1)} %copy-done.10, f32[8,64]{1,0:T(8,128)S(1)} %broadcast_multiply_fusion.2, f32[8,64]{1,0:T(8,128)S(1)} %copy-done.43, ...), kind=kLoop, calls=%fused_computation.134 | loop fusion | flops 153092096 | bytes 50991104 | tf_op jit(solution)/shard_map/broadcast_in_dim | solution.py:238
  570.9 48.6 %reduce-scatter.5.cloned.1.call-done = bf16[1024,512]{1,0:T(8,128)(2,1)} async-done(((bf16[4096,512]{1,0:T(8,128)(2,1)}), bf16[1024,512]{1,0:T(8,128)(2,1)}) %reduce-scatter.5.cloned.1.call-update) | async-done | bytes 1048592 | tf_op jit(solution)/shard_map/weight_grad/reduce_scatter | solution.py:225
  (263 shorter events, 218.4 us)
Async XLA Ops:
  7.2 155.7 %all-gather.3.cloned.1.call-start = ((), (), s32[]{:S(2)}) async-start(), calls=%async_computation.4 | async-start | bytes 10485760 | tf_op jit(solution)/shard_map/all_gather | solution.py:67
  10.3 560.6 %reduce-scatter.3.cloned.1.call-start = ((), (), s32[]{:S(2)}) async-start(), calls=%async_computation.2 | async-start | bytes 5242880 | tf_op jit(solution)/shard_map/weight_grad/reduce_scatter | solution.py:225
  22.1 74.3 %collective-permute-start.1 = (bf16[512,4096]{1,0:T(8,128)(2,1)S(1)}, bf16[512,4096]{1,0:T(8,128)(2,1)S(1)}, u32[]{:S(2)}, u32[]{:S(2)}) collective-permute-start(bf16[512,4096]{1,0:T(8,128)(2,1)S(1)} %bitcast.109), channel_id=1, source_target_pairs={{0,8},{8,0},{16,24},{24,16},{1,9},{9,1},{17,25},{25,17},{2,10},{10... | collective-permute-start | bytes 12582920 | tf_op jit(solution)/shard_map/phase_a/ppermute | solution.py:55
  27.5 74.5 %collective-permute-start.4 = (bf16[512,4096]{1,0:T(8,128)(2,1)S(1)}, bf16[512,4096]{1,0:T(8,128)(2,1)S(1)}, u32[]{:S(2)}, u32[]{:S(2)}) collective-permute-start(bf16[512,4096]{1,0:T(8,128)(2,1)S(1)} %bitcast.110), channel_id=1, source_target_pairs={{0,16},{8,24},{16,0},{24,8},{1,17},{9,25},{17,1},{25,9},{2,18},{10... | collective-permute-start | bytes 12582920 | tf_op jit(solution)/shard_map/phase_a/ppermute | solution.py:55
  98.0 28.3 %collective-permute-start.7 = (bf16[256,4096]{1,0:T(8,128)(2,1)}, bf16[256,4096]{1,0:T(8,128)(2,1)}, u32[]{:S(2)}, u32[]{:S(2)}) collective-permute-start(bf16[256,4096]{1,0:T(8,128)(2,1)} %slice.148), channel_id=1, source_target_pairs={{0,16},{8,24},{16,0},{24,8},{1,17},{9,25},{17,1},{25,9},{2,18},{10... | collective-permute-start | bytes 6291464 | tf_op jit(solution)/shard_map/phase_a/ppermute | solution.py:55
  105.5 85.7 %collective-permute-start.8 = (bf16[256,4096]{1,0:T(8,128)(2,1)}, bf16[256,4096]{1,0:T(8,128)(2,1)S(1)}, u32[]{:S(2)}, u32[]{:S(2)}) collective-permute-start(bf16[256,4096]{1,0:T(8,128)(2,1)} %slice.149), channel_id=1, source_target_pairs={{0,8},{8,0},{16,24},{24,16},{1,9},{9,1},{17,25},{25,17},{2,10},{10... | collective-permute-start | bytes 6291464 | tf_op jit(solution)/shard_map/phase_a/ppermute | solution.py:55
  112.9 49.9 %collective-permute-start = (bf16[512,1024]{1,0:T(8,128)(2,1)}, bf16[512,1024]{1,0:T(8,128)(2,1)}, u32[]{:S(2)}, u32[]{:S(2)}) collective-permute-start(bf16[512,1024]{1,0:T(8,128)(2,1)} %get-tuple-element.262), channel_id=1, source_target_pairs={{4,28},{12,20},{20,12},{28,4},{5,29},{13,21},{21,13},{29,5},{6,30}... | collective-permute-start | bytes 3145736 | tf_op jit(solution)/shard_map/phase_a/ppermute | solution.py:55
  114.6 62.4 %collective-permute-start.3 = (bf16[512,1024]{1,0:T(8,128)(2,1)}, bf16[512,1024]{1,0:T(8,128)(2,1)}, u32[]{:S(2)}, u32[]{:S(2)}) collective-permute-start(bf16[512,1024]{1,0:T(8,128)(2,1)} %get-tuple-element.261), channel_id=1, source_target_pairs={{4,12},{12,4},{20,28},{28,20},{5,13},{13,5},{21,29},{29,21},{6,14}... | collective-permute-start | bytes 3145736 | tf_op jit(solution)/shard_map/phase_a/ppermute | solution.py:55
  116.3 76.4 %collective-permute-start.6 = (bf16[512,1024]{1,0:T(8,128)(2,1)}, bf16[512,1024]{1,0:T(8,128)(2,1)}, u32[]{:S(2)}, u32[]{:S(2)}) collective-permute-start(bf16[512,1024]{1,0:T(8,128)(2,1)} %get-tuple-element.260), channel_id=1, source_target_pairs={{4,20},{12,28},{20,4},{28,12},{5,21},{13,29},{21,5},{29,13},{6,22}... | collective-permute-start | bytes 3145736 | tf_op jit(solution)/shard_map/phase_a/ppermute | solution.py:55
  173.7 41.6 %collective-permute-start.2 = (bf16[512,1024]{1,0:T(8,128)(2,1)}, bf16[512,1024]{1,0:T(8,128)(2,1)}, u32[]{:S(2)}, u32[]{:S(2)}) collective-permute-start(bf16[512,1024]{1,0:T(8,128)(2,1)} %get-tuple-element.221), channel_id=1, source_target_pairs={{0,8},{8,0},{16,24},{24,16},{1,9},{9,1},{17,25},{25,17},{2,10},{10... | collective-permute-start | bytes 3145736 | tf_op jit(solution)/shard_map/phase_a/ppermute | solution.py:62
  187.8 30.3 %collective-permute-start.5 = (bf16[512,1024]{1,0:T(8,128)(2,1)}, bf16[512,1024]{1,0:T(8,128)(2,1)}, u32[]{:S(2)}, u32[]{:S(2)}) collective-permute-start(bf16[512,1024]{1,0:T(8,128)(2,1)} %get-tuple-element.222), channel_id=1, source_target_pairs={{0,16},{8,24},{16,0},{24,8},{1,17},{9,25},{17,1},{25,9},{2,18},{10... | collective-permute-start | bytes 3145736 | tf_op jit(solution)/shard_map/phase_a/ppermute | solution.py:62
  202.5 17.6 %collective-permute-start.9 = (bf16[512,1024]{1,0:T(8,128)(2,1)S(1)}, bf16[512,1024]{1,0:T(8,128)(2,1)S(1)}, u32[]{:S(2)}, u32[]{:S(2)}) collective-permute-start(bf16[512,1024]{1,0:T(8,128)(2,1)S(1)} %get-tuple-element.223), channel_id=1, source_target_pairs={{0,24},{8,16},{16,8},{24,0},{1,25},{9,17},{17,9},{25,1},{2,26},{10... | collective-permute-start | bytes 3145736 | tf_op jit(solution)/shard_map/phase_a/ppermute | solution.py:62
  235.1 17.2 %collective-permute-start.14 = (bf16[256,4096]{1,0:T(8,128)(2,1)S(1)}, bf16[256,4096]{1,0:T(8,128)(2,1)S(1)}, u32[]{:S(2)}, u32[]{:S(2)}) collective-permute-start(bf16[256,4096]{1,0:T(8,128)(2,1)S(1)} %get-tuple-element.257), channel_id=1, source_target_pairs={{4,12},{12,4},{20,28},{28,20},{5,13},{13,5},{21,29},{29,21},{6,14}... | collective-permute-start | bytes 6291464 | tf_op jit(solution)/shard_map/phase_a/ppermute | solution.py:62
  236.0 18.1 %collective-permute-start.16 = (bf16[256,4096]{1,0:T(8,128)(2,1)S(1)}, bf16[256,4096]{1,0:T(8,128)(2,1)S(1)}, u32[]{:S(2)}, u32[]{:S(2)}) collective-permute-start(bf16[256,4096]{1,0:T(8,128)(2,1)S(1)} %get-tuple-element.258), channel_id=1, source_target_pairs={{4,20},{12,28},{20,4},{28,12},{5,21},{13,29},{21,5},{29,13},{6,22}... | collective-permute-start | bytes 6291464 | tf_op jit(solution)/shard_map/phase_a/ppermute | solution.py:62
  237.1 18.9 %collective-permute-start.18 = (bf16[256,4096]{1,0:T(8,128)(2,1)S(1)}, bf16[256,4096]{1,0:T(8,128)(2,1)}, u32[]{:S(2)}, u32[]{:S(2)}) collective-permute-start(bf16[256,4096]{1,0:T(8,128)(2,1)S(1)} %slice.136), channel_id=1, source_target_pairs={{4,20},{12,28},{20,4},{28,12},{5,21},{13,29},{21,5},{29,13},{6,22}... | collective-permute-start | bytes 6291464 | tf_op jit(solution)/shard_map/phase_a/ppermute | solution.py:62
  239.3 16.7 %collective-permute-start.13 = (bf16[256,4096]{1,0:T(8,128)(2,1)S(1)}, bf16[256,4096]{1,0:T(8,128)(2,1)}, u32[]{:S(2)}, u32[]{:S(2)}) collective-permute-start(bf16[256,4096]{1,0:T(8,128)(2,1)S(1)} %slice.130), channel_id=1, source_target_pairs={{4,12},{12,4},{20,28},{28,20},{5,13},{13,5},{21,29},{29,21},{6,14}... | collective-permute-start | bytes 6291464 | tf_op jit(solution)/shard_map/phase_a/ppermute | solution.py:62
  286.5 51.9 %collective-permute-start.19 = (bf16[8,64,4096]{2,1,0:T(8,128)(2,1)S(1)}, bf16[8,64,4096]{2,1,0:T(8,128)(2,1)S(1)}, u32[]{:S(2)}, u32[]{:S(2)}) collective-permute-start(bf16[8,64,4096]{2,1,0:T(8,128)(2,1)S(1)} %fusion.67), channel_id=1, source_target_pairs={{4,0},{5,1},{6,2},{7,3},{12,8},{13,9},{14,10},{15,11},{20,16},{21,... | collective-permute-start | bytes 12582920 | tf_op jit(solution)/shard_map/phase_a/ppermute | solution.py:200
  289.6 101.2 %collective-permute-start.27 = (bf16[256,4096]{1,0:T(8,128)(2,1)S(1)}, bf16[256,4096]{1,0:T(8,128)(2,1)S(1)}, u32[]{:S(2)}, u32[]{:S(2)}) collective-permute-start(bf16[256,4096]{1,0:T(8,128)(2,1)S(1)} %slice.150), channel_id=1, source_target_pairs={{4,20},{12,28},{20,4},{28,12},{5,21},{13,29},{21,5},{29,13},{6,22}... | collective-permute-start | bytes 6291464 | tf_op jit(solution)/shard_map/phase_a/ppermute | solution.py:55
  292.2 100.1 %collective-permute-start.28 = (bf16[256,4096]{1,0:T(8,128)(2,1)S(1)}, bf16[256,4096]{1,0:T(8,128)(2,1)S(1)}, u32[]{:S(2)}, u32[]{:S(2)}) collective-permute-start(bf16[256,4096]{1,0:T(8,128)(2,1)S(1)} %slice.151), channel_id=1, source_target_pairs={{4,12},{12,4},{20,28},{28,20},{5,13},{13,5},{21,29},{29,21},{6,14}... | collective-permute-start | bytes 6291464 | tf_op jit(solution)/shard_map/phase_a/ppermute | solution.py:55
  340.5 28.8 %collective-permute-start.20 = (bf16[512,1024]{1,0:T(8,128)(2,1)S(1)}, bf16[512,1024]{1,0:T(8,128)(2,1)S(1)}, u32[]{:S(2)}, u32[]{:S(2)}) collective-permute-start(bf16[512,1024]{1,0:T(8,128)(2,1)S(1)} %get-tuple-element.254), channel_id=1, source_target_pairs={{0,24},{8,16},{16,8},{24,0},{1,25},{9,17},{17,9},{25,1},{2,26},{10... | collective-permute-start | bytes 3145736 | tf_op jit(solution)/shard_map/phase_a/ppermute | solution.py:55
  343.7 47.1 %collective-permute-start.21 = (bf16[512,1024]{1,0:T(8,128)(2,1)S(1)}, bf16[512,1024]{1,0:T(8,128)(2,1)S(1)}, u32[]{:S(2)}, u32[]{:S(2)}) collective-permute-start(bf16[512,1024]{1,0:T(8,128)(2,1)S(1)} %get-tuple-element.253), channel_id=1, source_target_pairs={{0,8},{8,0},{16,24},{24,16},{1,9},{9,1},{17,25},{25,17},{2,10},{10... | collective-permute-start | bytes 3145736 | tf_op jit(solution)/shard_map/phase_a/ppermute | solution.py:55
  346.3 44.5 %collective-permute-start.24 = (bf16[512,1024]{1,0:T(8,128)(2,1)S(1)}, bf16[512,1024]{1,0:T(8,128)(2,1)S(1)}, u32[]{:S(2)}, u32[]{:S(2)}) collective-permute-start(bf16[512,1024]{1,0:T(8,128)(2,1)S(1)} %get-tuple-element.252), channel_id=1, source_target_pairs={{0,16},{8,24},{16,0},{24,8},{1,17},{9,25},{17,1},{25,9},{2,18},{10... | collective-permute-start | bytes 3145736 | tf_op jit(solution)/shard_map/phase_a/ppermute | solution.py:55
  410.7 208.8 %reduce-scatter.5.cloned.1.call-start = ((), (), s32[]{:S(2)}) async-start(), calls=%async_computation.3 | async-start | bytes 5242880 | tf_op jit(solution)/shard_map/weight_grad/reduce_scatter | solution.py:225
  421.3 37.5 %collective-permute-start.35 = (bf16[256,4096]{1,0:T(8,128)(2,1)}, bf16[256,4096]{1,0:T(8,128)(2,1)}, u32[]{:S(2)}, u32[]{:S(2)}) collective-permute-start(bf16[256,4096]{1,0:T(8,128)(2,1)} %get-tuple-element.250), channel_id=1, source_target_pairs={{0,16},{8,24},{16,0},{24,8},{1,17},{9,25},{17,1},{25,9},{2,18},{10... | collective-permute-start | bytes 6291464 | tf_op jit(solution)/shard_map/phase_b/ppermute | solution.py:62
  424.7 40.7 %collective-permute-start.33 = (bf16[256,4096]{1,0:T(8,128)(2,1)}, bf16[256,4096]{1,0:T(8,128)(2,1)}, u32[]{:S(2)}, u32[]{:S(2)}) collective-permute-start(bf16[256,4096]{1,0:T(8,128)(2,1)} %get-tuple-element.249), channel_id=1, source_target_pairs={{0,8},{8,0},{16,24},{24,16},{1,9},{9,1},{17,25},{25,17},{2,10},{10... | collective-permute-start | bytes 6291464 | tf_op jit(solution)/shard_map/phase_b/ppermute | solution.py:62
  437.8 34.1 %collective-permute-start.23 = (bf16[512,1024]{1,0:T(8,128)(2,1)}, bf16[512,1024]{1,0:T(8,128)(2,1)}, u32[]{:S(2)}, u32[]{:S(2)}) collective-permute-start(bf16[512,1024]{1,0:T(8,128)(2,1)} %get-tuple-element.230), channel_id=1, source_target_pairs={{4,12},{12,4},{20,28},{28,20},{5,13},{13,5},{21,29},{29,21},{6,14}... | collective-permute-start | bytes 3145736 | tf_op jit(solution)/shard_map/phase_b/ppermute | solution.py:62
  449.7 34.9 %collective-permute-start.26 = (bf16[512,1024]{1,0:T(8,128)(2,1)}, bf16[512,1024]{1,0:T(8,128)(2,1)}, u32[]{:S(2)}, u32[]{:S(2)}) collective-permute-start(bf16[512,1024]{1,0:T(8,128)(2,1)} %get-tuple-element.231), channel_id=1, source_target_pairs={{4,20},{12,28},{20,4},{28,12},{5,21},{13,29},{21,5},{29,13},{6,22}... | collective-permute-start | bytes 3145736 | tf_op jit(solution)/shard_map/phase_b/ppermute | solution.py:62
  454.6 60.8 %collective-permute-start.32 = (bf16[256,4096]{1,0:T(8,128)(2,1)}, bf16[256,4096]{1,0:T(8,128)(2,1)}, u32[]{:S(2)}, u32[]{:S(2)}) collective-permute-start(bf16[256,4096]{1,0:T(8,128)(2,1)} %slice.140), channel_id=1, source_target_pairs={{0,8},{8,0},{16,24},{24,16},{1,9},{9,1},{17,25},{25,17},{2,10},{10... | collective-permute-start | bytes 6291464 | tf_op jit(solution)/shard_map/phase_b/ppermute | solution.py:62
  458.8 56.7 %collective-permute-start.37 = (bf16[256,4096]{1,0:T(8,128)(2,1)}, bf16[256,4096]{1,0:T(8,128)(2,1)}, u32[]{:S(2)}, u32[]{:S(2)}) collective-permute-start(bf16[256,4096]{1,0:T(8,128)(2,1)} %slice.146), channel_id=1, source_target_pairs={{0,16},{8,24},{16,0},{24,8},{1,17},{9,25},{17,1},{25,9},{2,18},{10... | collective-permute-start | bytes 6291464 | tf_op jit(solution)/shard_map/phase_b/ppermute | solution.py:62
  465.4 51.2 %collective-permute-start.36 = (bf16[256,4096]{1,0:T(8,128)(2,1)}, bf16[256,4096]{1,0:T(8,128)(2,1)}, u32[]{:S(2)}, u32[]{:S(2)}) collective-permute-start(bf16[256,4096]{1,0:T(8,128)(2,1)} %add_convert_fusion.1), channel_id=1, source_target_pairs={{0,8},{8,0},{16,24},{24,16},{1,9},{9,1},{17,25},{25,17},{2,10},{10... | collective-permute-start | bytes 6291464 | tf_op jit(solution)/shard_map/phase_b/ppermute | solution.py:62
  472.0 48.8 %collective-permute-start.34 = (bf16[256,4096]{1,0:T(8,128)(2,1)}, bf16[256,4096]{1,0:T(8,128)(2,1)}, u32[]{:S(2)}, u32[]{:S(2)}) collective-permute-start(bf16[256,4096]{1,0:T(8,128)(2,1)} %add_convert_fusion.3), channel_id=1, source_target_pairs={{0,16},{8,24},{16,0},{24,8},{1,17},{9,25},{17,1},{25,9},{2,18},{10... | collective-permute-start | bytes 6291464 | tf_op jit(solution)/shard_map/phase_b/ppermute | solution.py:62
  484.5 28.6 %collective-permute-start.29 = (bf16[512,1024]{1,0:T(8,128)(2,1)}, bf16[512,1024]{1,0:T(8,128)(2,1)}, u32[]{:S(2)}, u32[]{:S(2)}) collective-permute-start(bf16[512,1024]{1,0:T(8,128)(2,1)} %get-tuple-element.232), channel_id=1, source_target_pairs={{4,28},{12,20},{20,12},{28,4},{5,29},{13,21},{21,13},{29,5},{6,30}... | collective-permute-start | bytes 3145736 | tf_op jit(solution)/shard_map/phase_b/ppermute | solution.py:62
  (63 other events, 777.0 us)
Sparse Core Ops, SparseCore 0:
  10.5 152.3 all-gather.2
  410.8 109.8 reduce-scatter.2
  523.0 96.4 reduce-scatter.4
